TPU v7x, 256 devices: a whole 4x4x8 slice. The times are simulated.
256 devices in a mesh: roll: 4 (over z_lo, core), mach: 16 (over y, x), cross: 4 (over z_hi).
Axes of the slice: x: 4, y: 4, z: 8 (z_hi: 4, z_lo: 2; z = z_hi * 2 + z_lo), core: 2. Of those that a mesh axis runs over, the one named last changes fastest.
Arguments:
- density: bfloat16 [128, 4096, 2048], P('roll', 'mach', 'cross'), may hold values from 0 to 1
- roll_start: float32 [32, 128], P(None, 'roll'), may hold values from 0.05 to 1
- mach_factor: bfloat16 [32, 4096], P(None, 'mach'), may hold values from 0.0099487305 to 1
- cross_factor: bfloat16 [32, 2048], P(None, 'cross'), may hold values from 0.0099487305 to 1
Outputs:
- roll_factor: float32 [32, 128], P(None, 'roll')
- mode_two: float32 [32, 4096], P(None, ('mach', 'cross'))
All inputs are finite; a program needn't handle non-finite values.
Results may differ from a plain program's by a relative error of at most 0.0003.
Values sent between devices are 32-bit elements; how exact they have to be, the bound alone decides.
A program may use at most 64 MiB of HBM per device.

v0:
```python
import jax
import jax.numpy as jnp
from jax import lax
from jax.sharding import PartitionSpec as P


def hals_rows(roll_rows, mttkrp, gram):

    def column_step(column, rows):
        column = jnp.asarray(column).astype(jnp.int32)
        gram_row = lax.dynamic_slice_in_dim(gram, column, 1, 0)
        diag_entry = lax.dynamic_slice_in_dim(gram_row, column, 1, 1)
        current = lax.dynamic_slice_in_dim(rows, column, 1, 0)
        target = lax.dynamic_slice_in_dim(mttkrp, column, 1, 0)
        mixed = jnp.dot(gram_row, rows, precision=lax.Precision.HIGHEST)
        updated = jnp.maximum(current + (target - mixed) / diag_entry, 0.0)
        return lax.dynamic_update_slice_in_dim(rows, updated, column, 0)

    return lax.fori_loop(0, roll_rows.shape[0], column_step, roll_rows)


def local(density, roll_start, mach_factor, cross_factor):
    rolls_here, bins_here, cross_here = density.shape
    rank = cross_factor.shape[0]
    flat = density.reshape(rolls_here * bins_here, cross_here)
    partial_value = lax.dot_general(
        cross_factor, flat, (((1,), (1,)), ((), ())), preferred_element_type=jnp.float32
    )
    partial_value = partial_value.reshape(rank, rolls_here, bins_here)
    local_terms = jnp.einsum(
        "rij,rj->ri",
        partial_value,
        mach_factor.astype(jnp.float32),
        precision=lax.Precision.HIGHEST,
    )
    local_mach = jnp.dot(mach_factor, mach_factor.T, preferred_element_type=jnp.float32)
    local_cross = jnp.dot(cross_factor, cross_factor.T, preferred_element_type=jnp.float32)
    mttkrp = lax.psum(local_terms, ("mach", "cross"))
    gram_mach = lax.psum(local_mach, "mach")
    gram_cross = lax.psum(local_cross, "cross")
    gram = gram_mach * gram_cross
    roll_factor = hals_rows(roll_start, mttkrp, gram)
    term = jnp.einsum("rij,ri->rj", partial_value, roll_factor, precision=lax.Precision.HIGHEST)
    whole = lax.psum(term, ("roll", "cross"))
    span = whole.shape[1] // lax.axis_size("cross")
    total = lax.dynamic_slice_in_dim(whole, lax.axis_index("cross") * span, span, 1)
    all_rolls = rolls_here * lax.axis_size("roll")
    all_cross = cross_here * lax.axis_size("cross")
    scale = rank / (all_rolls * all_cross)
    mode_two = total * scale
    return (roll_factor, mode_two)


def solution(mesh):
    in_specs = (P("roll", "mach", "cross"), P(None, "roll"), P(None, "mach"), P(None, "cross"))
    out_specs = (P(None, "roll"), P(None, ("mach", "cross")))
    return jax.shard_map(local, mesh=mesh, in_specs=in_specs, out_specs=out_specs, check_vma=False)
```

profile of v0, /device:TPU:1, one launch (start us, length us, event | category | flops | bytes accessed | tf_op | source)
XLA Modules:
  0.0 584.9 jit_solution(14968535453906031717)
XLA Ops:
  0.7 0.7 copy-done
  1.4 5.9 %fusion.9 = f32[32,32,256]{2,0,1:T(8,128)S(1)} fusion(bf16[32,256,512]{2,1,0:T(8,128)(2,1)} %param.6, bf16[32,512]{1,0:T(8,128)(2,1)S(1)} %copy-done), kind=kOutput, calls=%fused_computation.12 | convolution fusion | flops 268435456 | bytes 9469952 | tf_op jit(solution)/shard_map/dot_general | solution.py:26
  7.3 1.2 fusion.7
  8.5 327.1 %psum.28 = f32[32,32]{1,0:T(8,128)S(1)} all-reduce(f32[32,32]{1,0:T(8,128)S(1)} %bitcast.34), channel_id=1, replica_groups=mesh['roll'=4,'mach'=16,'cross'=4] {'mach','cross'}, use_global_device_ids=true, to_apply=%region_2.0 | all-reduce | flops 1024 | bytes 8192 | tf_op jit(solution)/shard_map/psum | solution.py:38
  335.7 56.2 %psum.29 = f32[32,32]{1,0:T(8,128)S(1)} all-reduce(f32[32,32]{1,0:T(8,128)S(1)} %fusion.12), channel_id=1, replica_groups=mesh['roll'=4,'mach'=16,'cross'=4] {'mach'}, use_global_device_ids=true, to_apply=%region_0.0 | all-reduce | flops 1024 | bytes 8192 | tf_op jit(solution)/shard_map/psum | solution.py:39
  392.0 12.7 %psum.30 = f32[32,32]{1,0:T(8,128)S(1)} all-reduce(f32[32,32]{1,0:T(8,128)S(1)} %fusion.13), channel_id=1, replica_groups=mesh['roll'=4,'mach'=16,'cross'=4] {'cross'}, use_global_device_ids=true, to_apply=%region_1.0 | all-reduce | flops 1024 | bytes 8192 | tf_op jit(solution)/shard_map/psum | solution.py:40
  404.7 45.2 %while.16 = (s32[]{:T(128)}, f32[32,32]{1,0:T(8,128)S(1)}, f32[32,32]{1,0:T(8,128)S(1)}, f32[32,32]{1,0:T(8,128)S(1)}, s32[]{:T(128)}, /*index=5*/s32[]{:T(128)}, s32[]{:T(128)}) while((s32[]{:T(128)}, f32[32,32]{1,0:T(8,128)S(1)}, f32[32,32]{1,0:T(8,128)S(1)}, f32[32,32]{1,0:T(8,128)S(1)}, s32[]{:T(128)}, /*index=5*/s32[]{:T(128)}, ...), condition=%wide.region_4.0_spmd, body=%wide.region_3.0_spmd.sunk | while | flops 12419 | bytes 19449 | solution.py:19
  404.7 0.6 dynamic_slice.66
  405.3 0.8 fusion.26
  406.1 0.6 dynamic_slice.66
  406.7 0.8 fusion.26
  407.6 0.6 dynamic_slice.66
  408.1 0.8 fusion.26
  409.0 0.6 dynamic_slice.66
  409.6 0.8 fusion.26
  410.4 0.6 dynamic_slice.66
  411.0 0.8 fusion.26
  411.8 0.6 dynamic_slice.66
  412.4 0.8 fusion.26
  413.2 0.6 dynamic_slice.66
  413.8 0.8 fusion.26
  414.6 0.6 dynamic_slice.66
  415.2 0.8 fusion.26
  416.0 0.6 dynamic_slice.66
  416.6 0.8 fusion.26
  417.4 0.6 dynamic_slice.66
  418.0 0.8 fusion.26
  418.8 0.6 dynamic_slice.66
  419.4 0.8 fusion.26
  420.3 0.6 dynamic_slice.66
  420.8 0.8 fusion.26
  421.7 0.6 dynamic_slice.66
  422.3 0.8 fusion.26
  423.1 0.6 dynamic_slice.66
  423.7 0.8 fusion.26
  424.5 0.6 dynamic_slice.66
  425.1 0.8 fusion.26
  425.9 0.6 dynamic_slice.66
  426.5 0.8 fusion.26
  427.3 0.6 dynamic_slice.66
  427.9 0.8 fusion.26
  428.7 0.6 dynamic_slice.66
  429.3 0.8 fusion.26
  430.1 0.6 dynamic_slice.66
  430.7 0.8 fusion.26
  431.6 0.6 dynamic_slice.66
  432.1 0.8 fusion.26
  433.0 0.6 dynamic_slice.66
  433.6 0.8 fusion.26
  435.0 0.8 fusion.26
  436.4 0.8 fusion.26
  437.8 0.8 fusion.26
  439.2 0.8 fusion.26
  440.6 0.8 fusion.26
  442.0 0.8 fusion.26
  443.4 0.8 fusion.26
  444.8 0.8 fusion.26
  445.7 0.6 dynamic_slice.66
  446.3 0.8 fusion.26
  447.7 0.8 fusion.26
  449.1 0.8 fusion.26
  449.9 1.3 fusion.5
  451.2 133.1 %psum.31 = f32[32,256]{1,0:T(8,128)S(1)} all-reduce(f32[32,256]{1,0:T(8,128)S(1)} %bitcast.33), channel_id=1, replica_groups=mesh['roll'=4,'mach'=16,'cross'=4] {'roll','cross'}, use_global_device_ids=true, to_apply=%region_5.0 | all-reduce | flops 8192 | bytes 65536 | tf_op jit(solution)/shard_map/psum | solution.py:44
  584.3 0.7 dynamic-slice_multiply_fusion
  (53 shorter events, 7.0 us)
Async XLA Ops:
  0.6 0.8 copy-start
  0.6 404.1 %copy-start.2 = (f32[32,32]{1,0:T(8,128)S(1)}, f32[32,32]{1,0:T(8,128)}, u32[]{:S(2)}) copy-start(f32[32,32]{1,0:T(8,128)} %param.7) | copy-start | bytes 12292
  0.7 6.6 %copy-start.3 = (bf16[32,256]{1,0:T(8,128)(2,1)S(1)}, bf16[32,256]{1,0:T(8,128)(2,1)}, u32[]{:S(2)}) copy-start(bf16[32,256]{1,0:T(8,128)(2,1)} %param.8) | copy-start | bytes 49156
  449.9 135.0 %copy-start.1 = (f32[32,32]{1,0:T(8,128)}, f32[32,32]{1,0:T(8,128)S(1)}, u32[]{:S(2)}) copy-start(f32[32,32]{1,0:T(8,128)S(1)} %get-tuple-element.124) | copy-start | bytes 12292
where the time goes:
time: 585 us
  blocking collectives  529 us (90%)
  matrix products  33.6 us (6%)
  local copies, waits for them, and re-layouts  20.4 us (3%)
    psum x1, blocking collectives, local(): mttkrp = lax.psum(local_terms, ('mach', 'cross'))  327 us
    psum x1, blocking collectives, local(): whole = lax.psum(term, ('roll', 'cross'))  133 us
    psum x1, blocking collectives, local(): gram_mach = lax.psum(local_mach, 'mach')  56.2 us
    dot_general x32, matrix products, column_step(): mixed = jnp.dot(gram_row, rows, precision=lax.Precision.HIGHEST)  25 us
    dynamic_slice x32, local copies, waits for them, and re-layouts, column_step(): diag_entry = lax.dynamic_slice_in_dim(gram_row, column, 1, 1)  18.8 us
    psum x1, blocking collectives, local(): gram_cross = lax.psum(local_cross, 'cross')  12.7 us

commit v1 on v0

v1 whole, which is shorter than its diff:
```python
import jax
import jax.numpy as jnp
from jax import lax
from jax.sharding import PartitionSpec as P


def hals_rows(roll_rows, mttkrp, gram):
    def column_step(column, rows):
        column = jnp.asarray(column).astype(jnp.int32)
        gram_row = lax.dynamic_slice_in_dim(gram, column, 1, 0)
        diag_entry = lax.dynamic_slice_in_dim(gram_row, column, 1, 1)
        current = lax.dynamic_slice_in_dim(rows, column, 1, 0)
        target = lax.dynamic_slice_in_dim(mttkrp, column, 1, 0)
        mixed = jnp.dot(gram_row, rows, precision=lax.Precision.HIGHEST)
        updated = jnp.maximum(current + (target - mixed) / diag_entry, 0.0)
        return lax.dynamic_update_slice_in_dim(rows, updated, column, 0)
    return lax.fori_loop(0, roll_rows.shape[0], column_step, roll_rows)


def local(density, roll_start, mach_factor, cross_factor):
    rolls_here, bins_here, cross_here = density.shape
    rank = cross_factor.shape[0]
    flat = density.reshape(rolls_here * bins_here, cross_here)
    partial_value = lax.dot_general(cross_factor, flat, (((1,), (1,)), ((), ())), preferred_element_type=jnp.float32)
    partial_value = partial_value.reshape(rank, rolls_here, bins_here)
    local_terms = jnp.einsum("rij,rj->ri", partial_value, mach_factor.astype(jnp.float32), precision=lax.Precision.HIGHEST)
    local_mach = jnp.dot(mach_factor, mach_factor.T, preferred_element_type=jnp.float32)
    local_cross = jnp.dot(cross_factor, cross_factor.T, preferred_element_type=jnp.float32)
    a = lax.axis_index("roll"); m = lax.axis_index("mach"); c = lax.axis_index("cross")
    nroll = lax.axis_size("roll")
    slots = jnp.zeros((nroll + 2, rank, rank), jnp.float32)
    slots = lax.dynamic_update_slice_in_dim(slots, local_terms[None], a, 0)
    slots = slots.at[nroll].set(jnp.where((a == 0) & (c == 0), local_mach, 0.0))
    slots = slots.at[nroll + 1].set(jnp.where((a == 0) & (m == 0), local_cross, 0.0))
    tot = lax.psum(slots, ("roll", "mach", "cross"))
    mttkrp = lax.dynamic_index_in_dim(tot, a, 0, keepdims=False)
    gram = tot[nroll] * tot[nroll + 1]
    roll_factor = hals_rows(roll_start, mttkrp, gram)
    term = jnp.einsum("rij,ri->rj", partial_value, roll_factor, precision=lax.Precision.HIGHEST)
    nm = lax.axis_size("mach")
    ms = jnp.zeros((nm,) + term.shape, jnp.float32)
    ms = lax.dynamic_update_slice_in_dim(ms, term[None], m, 0)
    whole = lax.psum(ms, ("roll", "mach", "cross"))
    whole = lax.dynamic_index_in_dim(whole, m, 0, keepdims=False)
    span = whole.shape[1] // lax.axis_size("cross")
    total = lax.dynamic_slice_in_dim(whole, c * span, span, 1)
    scale = rank / (rolls_here * nroll * cross_here * lax.axis_size("cross"))
    return (roll_factor, total * scale)


def solution(mesh):
    in_specs = (P("roll", "mach", "cross"), P(None, "roll"), P(None, "mach"), P(None, "cross"))
    out_specs = (P(None, "roll"), P(None, ("mach", "cross")))
    return jax.shard_map(local, mesh=mesh, in_specs=in_specs, out_specs=out_specs, check_vma=False)
```

time: 585 us -> 400 us (0.68)
  blocking collectives: 529 us -> 81.8 us
  waiting for transfers between devices: 0 us -> 246 us
  between operations: 0.71 us -> 14.2 us
    psum x4 -> x1, blocking collectives: 529 us -> 81.8 us  [local(): tot = lax.psum(slots, ('roll', 'mach', 'cross'))]
    psum x0 -> x1, waiting for transfers between devices: none -> 246 us  [local(): whole = lax.psum(ms, ('roll', 'mach', 'cross'))]
  transfers between devices with their start and end apart: 0 -> 1, of which waited for: 0 -> 1; matrix products, arithmetic and copies ran while one was open for 0% -> 0% of each run, Pallas kernels for 0% -> 0%
where the time goes in v1:
time: 400 us; the launch traced here: 399 us
  waiting for transfers between devices  246 us (62%)
  blocking collectives  81.8 us (20%)
  matrix products  33.6 us (8%)
  local copies, waits for them, and re-layouts  21.2 us (5%)
  between operations  14.2 us (4%)
    psum x1, waiting for transfers between devices, local(): whole = lax.psum(ms, ('roll', 'mach', 'cross'))  246 us
    psum x1, blocking collectives, local(): tot = lax.psum(slots, ('roll', 'mach', 'cross'))  81.8 us
    dot_general x32, matrix products, column_step(): mixed = jnp.dot(gram_row, rows, precision=lax.Precision.HIGHEST)  25 us
    dynamic_slice x32, local copies, waits for them, and re-layouts, column_step(): diag_entry = lax.dynamic_slice_in_dim(gram_row, column, 1, 1)  18.8 us
  transfers between devices with their start and end apart: 1, of which 1 were waited for; matrix products, arithmetic and copies ran while one was open for 0% of the time, Pallas kernels for 0%

profile of v1, /device:TPU:1, one launch (start us, length us, event | category | flops | bytes accessed | tf_op | source)
XLA Modules:
  0.0 398.7 jit_solution(10247666444916578830)
XLA Ops:
  7.3 0.7 copy-done
  7.9 5.9 %fusion.13 = f32[32,32,256]{2,0,1:T(8,128)S(1)} fusion(bf16[32,256,512]{2,1,0:T(8,128)(2,1)} %param.10, bf16[32,512]{1,0:T(8,128)(2,1)S(1)} %copy-done), kind=kOutput, calls=%fused_computation.19 | convolution fusion | flops 268435456 | bytes 9469952 | tf_op jit(solution)/shard_map/dot_general | solution.py:24
  13.8 1.2 fusion.11
  15.3 81.8 %psum.14 = f32[6,32,32]{2,1,0:T(8,128)S(1)} all-reduce(f32[6,32,32]{2,1,0:T(8,128)S(1)} %fusion.6), channel_id=1, replica_groups=mesh['roll'=4,'mach'=16,'cross'=4] {'roll','mach','cross'}, use_global_device_ids=true, to_apply=%region_0.1 | all-reduce | flops 6144 | bytes 49152 | tf_op jit(solution)/shard_map/psum | solution.py:35
  97.1 45.2 %while.18 = (s32[]{:T(128)}, f32[32,32]{1,0:T(8,128)S(1)}, f32[32,32]{1,0:T(8,128)S(1)}, f32[32,32]{1,0:T(8,128)S(1)}, s32[]{:T(128)}, /*index=5*/s32[]{:T(128)}, s32[]{:T(128)}) while((s32[]{:T(128)}, f32[32,32]{1,0:T(8,128)S(1)}, f32[32,32]{1,0:T(8,128)S(1)}, f32[32,32]{1,0:T(8,128)S(1)}, s32[]{:T(128)}, /*index=5*/s32[]{:T(128)}, ...), condition=%wide.region_2.3_spmd, body=%wide.region_1.2_spmd.sunk | while | flops 12419 | bytes 19949 | solution.py:17
  97.1 0.6 dynamic_slice.74
  97.7 0.8 fusion.29
  98.5 0.6 dynamic_slice.74
  99.1 0.8 fusion.29
  100.0 0.6 dynamic_slice.74
  100.5 0.8 fusion.29
  101.4 0.6 dynamic_slice.74
  102.0 0.8 fusion.29
  102.8 0.6 dynamic_slice.74
  103.4 0.8 fusion.29
  104.2 0.6 dynamic_slice.74
  104.8 0.8 fusion.29
  105.6 0.6 dynamic_slice.74
  106.2 0.8 fusion.29
  107.0 0.6 dynamic_slice.74
  107.6 0.8 fusion.29
  108.4 0.6 dynamic_slice.74
  109.0 0.8 fusion.29
  109.8 0.6 dynamic_slice.74
  110.4 0.8 fusion.29
  111.3 0.6 dynamic_slice.74
  111.8 0.8 fusion.29
  112.7 0.6 dynamic_slice.74
  113.3 0.8 fusion.29
  114.1 0.6 dynamic_slice.74
  114.7 0.8 fusion.29
  115.5 0.6 dynamic_slice.74
  116.1 0.8 fusion.29
  116.9 0.6 dynamic_slice.74
  117.5 0.8 fusion.29
  118.3 0.6 dynamic_slice.74
  118.9 0.8 fusion.29
  119.7 0.6 dynamic_slice.74
  120.3 0.8 fusion.29
  121.1 0.6 dynamic_slice.74
  121.7 0.8 fusion.29
  122.5 0.6 dynamic_slice.74
  123.1 0.8 fusion.29
  124.0 0.6 dynamic_slice.74
  124.5 0.8 fusion.29
  125.4 0.6 dynamic_slice.74
  126.0 0.8 fusion.29
  126.8 0.6 dynamic_slice.74
  127.4 0.8 fusion.29
  128.2 0.6 dynamic_slice.74
  128.8 0.8 fusion.29
  130.2 0.8 fusion.29
  131.6 0.8 fusion.29
  133.0 0.8 fusion.29
  134.4 0.8 fusion.29
  135.8 0.8 fusion.29
  137.2 0.8 fusion.29
  138.7 0.8 fusion.29
  140.1 0.8 fusion.29
  141.5 0.8 fusion.29
  142.3 1.3 fusion.9
  143.7 0.8 copy-done.1
  144.5 245.9 %all-reduce.2.cloned.1.call-done = f32[16,32,256]{2,1,0:T(8,128)} async-done(((f32[16,32,256]{2,1,0:T(8,128)}), f32[16,32,256]{2,1,0:T(8,128)}) %all-reduce.2.cloned.1.call-update) | async-done | bytes 524304 | tf_op jit(solution)/shard_map/psum | solution.py:43
  390.4 1.4 multiply_bitcast_fusion
  (58 shorter events, 6.5 us)
Async XLA Ops:
  7.2 0.8 copy-start
  7.2 6.7 %copy-start.4 = (bf16[32,256]{1,0:T(8,128)(2,1)S(1)}, bf16[32,256]{1,0:T(8,128)(2,1)}, u32[]{:S(2)}) copy-start(bf16[32,256]{1,0:T(8,128)(2,1)} %param.12) | copy-start | bytes 49156
  7.2 89.9 %copy-start.3 = (f32[32,32]{1,0:T(8,128)S(1)}, f32[32,32]{1,0:T(8,128)}, u32[]{:S(2)}) copy-start(f32[32,32]{1,0:T(8,128)} %param.11) | copy-start | bytes 12292
  7.2 383.2 %all-reduce.2.cloned.1.call-start = ((), (), s32[]{:S(2)}) async-start(), calls=%async_computation | async-start | bytes 1048576 | tf_op jit(solution)/shard_map/psum | solution.py:43
  142.3 249.5 %copy-start.2 = (f32[32,32]{1,0:T(8,128)}, f32[32,32]{1,0:T(8,128)S(1)}, u32[]{:S(2)}) copy-start(f32[32,32]{1,0:T(8,128)S(1)} %get-tuple-element.148) | copy-start | bytes 12292
  143.6 0.8 copy-start.1
Sparse Core Ops, SparseCore 0:
  144.6 245.7 all-reduce.1

commit v2 on v0

v2 whole, which is shorter than its diff:
```python
import functools

import jax
import jax.numpy as jnp
from jax import lax
from jax.experimental import pallas as pl
from jax.experimental.pallas import tpu as pltpu
from jax.sharding import PartitionSpec as P

MESH = pl.DeviceIdType.MESH
VMEM = pltpu.VMEM


def gram_sum_kernel(n_cross, pay_ref, out_ref, recv, send_sem, recv_sem):
    roll = lax.axis_index("roll")
    mach = lax.axis_index("mach")
    cross = lax.axis_index("cross")
    group = recv.shape[0]
    n_mach = group // n_cross
    me = mach * n_cross + cross

    barrier = pltpu.get_barrier_semaphore()

    def greet(p, carry):
        @pl.when(p != me)
        def _():
            pl.semaphore_signal(barrier, inc=1, device_id=(roll, p // n_cross, p % n_cross), device_id_type=MESH)
        return carry

    lax.fori_loop(0, group, greet, 0)
    pl.semaphore_wait(barrier, group - 1)

    def each_peer(p, action):
        pm = p // n_cross
        pc = p % n_cross
        same_cross = jnp.logical_and(pc == cross, pm != mach)
        same_mach = jnp.logical_and(pm == mach, pc != cross)
        other = jnp.logical_and(pm != mach, pc != cross)

        @pl.when(same_cross)
        def _():
            action(p, 0, 16)

        @pl.when(same_mach)
        def _():
            action(p, 8, 16)

        @pl.when(other)
        def _():
            action(p, 8, 8)

    def start(p, lo, size):
        pltpu.make_async_remote_copy(
            src_ref=pay_ref.at[pl.ds(lo, size)],
            dst_ref=recv.at[me, pl.ds(lo, size)],
            send_sem=send_sem.at[p],
            recv_sem=recv_sem.at[me],
            device_id=(roll, p // n_cross, p % n_cross),
            device_id_type=MESH,
        ).start()

    def finish(p, lo, size):
        pltpu.make_async_remote_copy(
            src_ref=pay_ref.at[pl.ds(lo, size)],
            dst_ref=recv.at[p, pl.ds(lo, size)],
            send_sem=send_sem.at[p],
            recv_sem=recv_sem.at[p],
            device_id=(roll, p // n_cross, p % n_cross),
            device_id_type=MESH,
        ).wait()

    def send_loop(p, carry):
        each_peer(p, start)
        return carry

    def wait_loop(p, carry):
        each_peer(p, finish)
        return carry

    lax.fori_loop(0, group, send_loop, 0)
    recv[me] = pay_ref[...]
    lax.fori_loop(0, group, wait_loop, 0)

    terms = recv[0, 8:16, :]
    for p in range(1, group):
        terms = terms + recv[p, 8:16, :]
    gm = recv[cross, 0:8, :]
    for q in range(1, n_mach):
        gm = gm + recv[q * n_cross + cross, 0:8, :]
    gc = recv[mach * n_cross, 16:24, :]
    for q in range(1, n_cross):
        gc = gc + recv[mach * n_cross + q, 16:24, :]
    out_ref[0:8, :] = gm
    out_ref[8:16, :] = terms
    out_ref[16:24, :] = gc


def mode_sum_kernel(n_cross, scale, pieces_ref, out_ref, recv, send_sem, recv_sem):
    roll = lax.axis_index("roll")
    mach = lax.axis_index("mach")
    cross = lax.axis_index("cross")
    group = recv.shape[0]
    me = roll * n_cross + cross

    barrier = pltpu.get_barrier_semaphore()

    def greet(p, carry):
        @pl.when(p != me)
        def _():
            pl.semaphore_signal(barrier, inc=1, device_id=(p // n_cross, mach, p % n_cross), device_id_type=MESH)
        return carry

    lax.fori_loop(0, group, greet, 0)
    pl.semaphore_wait(barrier, group - 1)

    def send_loop(p, carry):
        @pl.when(p != me)
        def _():
            pltpu.make_async_remote_copy(
                src_ref=pieces_ref.at[p % n_cross],
                dst_ref=recv.at[me],
                send_sem=send_sem.at[p],
                recv_sem=recv_sem.at[me],
                device_id=(p // n_cross, mach, p % n_cross),
                device_id_type=MESH,
            ).start()
        return carry

    def wait_loop(p, carry):
        @pl.when(p != me)
        def _():
            pltpu.make_async_remote_copy(
                src_ref=pieces_ref.at[p % n_cross],
                dst_ref=recv.at[p],
                send_sem=send_sem.at[p],
                recv_sem=recv_sem.at[p],
                device_id=(p // n_cross, mach, p % n_cross),
                device_id_type=MESH,
            ).wait()
        return carry

    lax.fori_loop(0, group, send_loop, 0)
    recv[me] = pieces_ref[cross]
    lax.fori_loop(0, group, wait_loop, 0)

    total = recv[0]
    for p in range(1, group):
        total = total + recv[p]
    out_ref[...] = total * scale


def hals_kernel(sums_ref, start_ref, out_ref):
    gram = sums_ref[0] * sums_ref[2]
    target = sums_ref[1]
    out_ref[...] = start_ref[...]
    for r in range(out_ref.shape[0]):
        rows = out_ref[...]
        mixed = jnp.sum(gram[:, r : r + 1] * rows, axis=0, keepdims=True)
        current = rows[r : r + 1, :]
        updated = jnp.maximum(current + (target[r : r + 1, :] - mixed) / gram[r : r + 1, r : r + 1], 0.0)
        out_ref[r : r + 1, :] = updated


def local(density, roll_start, mach_factor, cross_factor):
    rolls_here, bins_here, cross_here = density.shape
    rank = cross_factor.shape[0]
    n_roll = lax.axis_size("roll")
    n_mach = lax.axis_size("mach")
    n_cross = lax.axis_size("cross")
    flat = density.reshape(rolls_here * bins_here, cross_here)
    partial_value = lax.dot_general(
        cross_factor, flat, (((1,), (1,)), ((), ())), preferred_element_type=jnp.float32
    )
    partial_value = partial_value.reshape(rank, rolls_here, bins_here)
    local_terms = jnp.einsum(
        "rij,rj->ri", partial_value, mach_factor.astype(jnp.float32), precision=lax.Precision.HIGHEST
    )
    local_mach = jnp.dot(mach_factor, mach_factor.T, preferred_element_type=jnp.float32)
    local_cross = jnp.dot(cross_factor, cross_factor.T, preferred_element_type=jnp.float32)
    pay = jnp.stack([local_mach, local_terms, local_cross]).reshape(24, 128)

    sums = pl.pallas_call(
        functools.partial(gram_sum_kernel, n_cross),
        out_shape=jax.ShapeDtypeStruct((24, 128), jnp.float32),
        in_specs=[pl.BlockSpec(memory_space=VMEM)],
        out_specs=pl.BlockSpec(memory_space=VMEM),
        scratch_shapes=[
            VMEM((n_mach * n_cross, 24, 128), jnp.float32),
            pltpu.SemaphoreType.DMA((n_mach * n_cross,)),
            pltpu.SemaphoreType.DMA((n_mach * n_cross,)),
        ],
        compiler_params=pltpu.CompilerParams(collective_id=0, has_side_effects=True),
    )(pay)
    sums = sums.reshape(3, rank, rank)

    roll_factor = pl.pallas_call(
        hals_kernel,
        out_shape=jax.ShapeDtypeStruct(roll_start.shape, jnp.float32),
        in_specs=[pl.BlockSpec(memory_space=VMEM)] * 2,
        out_specs=pl.BlockSpec(memory_space=VMEM),
    )(sums, roll_start)

    term = jnp.einsum("rij,ri->rj", partial_value, roll_factor, precision=lax.Precision.HIGHEST)
    span = bins_here // n_cross
    pieces = term.reshape(rank, n_cross, span).transpose(1, 0, 2).reshape(n_cross, rank * span // 128, 128)
    scale = rank / (rolls_here * n_roll * cross_here * n_cross)
    mode = pl.pallas_call(
        functools.partial(mode_sum_kernel, n_cross, scale),
        out_shape=jax.ShapeDtypeStruct(pieces.shape[1:], jnp.float32),
        in_specs=[pl.BlockSpec(memory_space=VMEM)],
        out_specs=pl.BlockSpec(memory_space=VMEM),
        scratch_shapes=[
            VMEM((n_roll * n_cross,) + pieces.shape[1:], jnp.float32),
            pltpu.SemaphoreType.DMA((n_roll * n_cross,)),
            pltpu.SemaphoreType.DMA((n_roll * n_cross,)),
        ],
        compiler_params=pltpu.CompilerParams(collective_id=1, has_side_effects=True),
    )(pieces)
    mode_two = mode.reshape(rank, span)
    return (roll_factor, mode_two)


def solution(mesh):
    in_specs = (P("roll", "mach", "cross"), P(None, "roll"), P(None, "mach"), P(None, "cross"))
    out_specs = (P(None, "roll"), P(None, ("mach", "cross")))
    return jax.shard_map(local, mesh=mesh, in_specs=in_specs, out_specs=out_specs, check_vma=False)
```

time: 585 us -> 51.9 us (0.09)
  the two profiles are of different devices: /device:TPU:1 before, /device:TPU:57 now
where the time goes in v2:
time: 51.9 us; the launch traced here: 51.3 us
  Pallas kernels  36.2 us (70%)
  matrix products  10.1 us (19%)
  local copies, waits for them, and re-layouts  4.25 us (8%)
  between operations  0.71 us (1%)
    pallas_call x1, Pallas kernels, local(): pl.pallas_call(functools.partial(gram_sum_kernel, n_cross), out_shape=jax...  20.7 us
    pallas_call x1, Pallas kernels, local(): pl.pallas_call(functools.partial(mode_sum_kernel, n_cross, scale), out_sh...  13.4 us
    dot_general x1, matrix products, local(): lax.dot_general(cross_factor, flat, (((1,), (1,)), ((), ())), preferred_e...  5.92 us
    pallas_call x1, Pallas kernels, local(): pl.pallas_call(hals_kernel, out_shape=jax.ShapeDtypeStruct(roll_start.sha...  2.12 us
    dot_general x1, matrix products, local(): jnp.einsum('rij,ri->rj', partial_value, roll_factor, precision=lax.Precis...  1.97 us
    reshape x1, local copies, waits for them, and re-layouts, local(): sums = sums.reshape(3, rank, rank)  1.4 us
    reshape x1, local copies, waits for them, and re-layouts, local(): mode_two = mode.reshape(rank, span)  1.37 us
    dot_general x1, matrix products, local(): jnp.einsum('rij,rj->ri', partial_value, mach_factor.astype(jnp.float32),...  1.18 us

profile of v2, /device:TPU:57, one launch (start us, length us, event | category | flops | bytes accessed | tf_op | source)
XLA Modules:
  0.0 51.3 jit_solution(15809353048790049724)
XLA Ops:
  0.6 0.0 copy-start
  0.6 0.0 copy-start.1
  0.7 0.9 %convolution_bitcast_fusion.1 = f32[1,32,32]{2,1,0:T(8,128)S(1)} fusion(bf16[32,256]{1,0:T(8,128)(2,1)} %param.6), kind=kOutput, calls=%fused_computation.1 | convolution fusion | flops 524288 | bytes 20480 | tf_op jit(solution)/shard_map/dot_general | solution.py:178
  1.6 0.0 copy-done
  1.6 0.1 convolution_bitcast_fusion
  1.7 5.9 %fusion.4 = f32[32,32,256]{2,0,1:T(8,128)S(1)} fusion(bf16[32,256,512]{2,1,0:T(8,128)(2,1)} %param.4, bf16[32,512]{1,0:T(8,128)(2,1)S(1)} %copy-done), kind=kOutput, calls=%fused_computation.7 | convolution fusion | flops 268435456 | bytes 9469952 | tf_op jit(solution)/shard_map/dot_general | solution.py:171
  7.6 0.0 copy-done.1
  7.7 1.2 %fusion.2 = f32[32,1,32]{2,1,0:T(1,128)S(1)} fusion(f32[32,32,256]{2,0,1:T(8,128)S(1)} %fusion.4, bf16[32,256,1]{1,0,2:T(8,128)(2,1)S(1)} %bitcast.24), kind=kOutput, calls=%fused_computation.4 | convolution fusion | flops 3145728 | bytes 1069056 | tf_op jit(solution)/shard_map/rij,rj->ri/dot_general | solution.py:175
  8.8 0.7 %reshape.23.pay_ref = f32[24,128]{1,0:T(8,128)} reshape(f32[3,32,32]{2,1,0:T(8,128)S(1)} %pad_maximum_fusion) | data formatting | bytes 24576 | tf_op jit(solution)/shard_map/reshape | solution.py:180
  9.5 20.7 %shard_map.59 = f32[24,128]{1,0:T(8,128)} custom-call(f32[24,128]{1,0:T(8,128)} %reshape.23.pay_ref), custom_call_target="tpu_custom_call" | custom-call | tf_op jit(solution)/shard_map/pallas_call | solution.py:182
  30.2 1.4 %reshape.24.sums_ref = f32[3,32,32]{2,1,0:T(8,128)} reshape(f32[24,128]{1,0:T(8,128)} %shard_map.59) | data formatting | bytes 24576 | tf_op jit(solution)/shard_map/reshape | solution.py:194
  31.6 2.1 %shard_map.60 = f32[32,32]{1,0:T(8,128)} custom-call(f32[3,32,32]{2,1,0:T(8,128)} %reshape.24.sums_ref, f32[32,32]{1,0:T(8,128)} %start_ref.1), custom_call_target="tpu_custom_call" | custom-call | tf_op jit(solution)/shard_map/pallas_call | solution.py:196
  33.7 2.0 %fusion = f32[32,1,256]{2,1,0:T(1,128)S(1)} fusion(f32[32,32,1]{1,2,0:T(1,128)} %bitcast.27, f32[32,32,256]{2,0,1:T(8,128)S(1)} %fusion.4), kind=kOutput, calls=%fused_computation.2 | convolution fusion | flops 3145728 | bytes 1085440 | tf_op jit(solution)/shard_map/rij,ri->rj/dot_general | solution.py:203
  35.7 0.1 reshape.25
  35.8 0.7 %reshape.26.pieces_ref = f32[4,16,128]{2,1,0:T(8,128)} reshape(f32[4,32,64]{2,1,0:T(8,128)S(1)} %copy.6) | data formatting | bytes 65536 | tf_op jit(solution)/shard_map/reshape | solution.py:205
  36.5 13.4 %shard_map.61 = f32[16,128]{1,0:T(8,128)} custom-call(f32[4,16,128]{2,1,0:T(8,128)} %reshape.26.pieces_ref), custom_call_target="tpu_custom_call" | custom-call | tf_op jit(solution)/shard_map/pallas_call | solution.py:207
  50.0 1.4 %reshape.27 = f32[32,64]{1,0:T(8,128)} reshape(f32[16,128]{1,0:T(8,128)} %shard_map.61) | data formatting | bytes 16384 | tf_op jit(solution)/shard_map/reshape | solution.py:219
  (3 shorter events, 0.0 us)
Async XLA Ops:
  0.6 1.0 %copy-start = (bf16[32,512]{1,0:T(8,128)(2,1)S(1)}, bf16[32,512]{1,0:T(8,128)(2,1)}, u32[]{:S(2)}) copy-start(bf16[32,512]{1,0:T(8,128)(2,1)} %param.7) | copy-start | bytes 98308
  0.6 7.0 %copy-start.1 = (bf16[32,256]{1,0:T(8,128)(2,1)S(1)}, bf16[32,256]{1,0:T(8,128)(2,1)}, u32[]{:S(2)}) copy-start(bf16[32,256]{1,0:T(8,128)(2,1)} %param.6) | copy-start | bytes 49156

commit v3 on v0

v3 whole, which is shorter than its diff:
```python
import functools

import jax
import jax.numpy as jnp
from jax import lax
from jax.experimental import pallas as pl
from jax.experimental.pallas import tpu as pltpu
from jax.sharding import PartitionSpec as P

MESH = pl.DeviceIdType.MESH
VMEM = pltpu.VMEM


def fused_kernel(n_roll, n_cross, scale, pay_ref, part_ref, start_ref, rf_ref, mode_ref,
                 recv_a, send_a, got_a, gm_s, mt_s, gc_s, term_s, pieces, recv_b, send_b, got_b, total_s):
    roll = lax.axis_index("roll")
    mach = lax.axis_index("mach")
    cross = lax.axis_index("cross")
    group_a = recv_a.shape[0]
    group_b = recv_b.shape[0]
    n_mach = group_a // n_cross
    me_a = mach * n_cross + cross
    me_b = roll * n_cross + cross
    rank = rf_ref.shape[0]

    def peer_a(p):
        return (roll, p // n_cross, p % n_cross)

    def peer_b(p):
        return (p // n_cross, mach, p % n_cross)

    barrier = pltpu.get_barrier_semaphore()

    def greet_a(p, carry):
        @pl.when(p != me_a)
        def _():
            pl.semaphore_signal(barrier, inc=1, device_id=peer_a(p), device_id_type=MESH)
        return carry

    def greet_b(p, carry):
        @pl.when(p // n_cross != roll)
        def _():
            pl.semaphore_signal(barrier, inc=1, device_id=peer_b(p), device_id_type=MESH)
        return carry

    lax.fori_loop(0, group_a, greet_a, 0)
    lax.fori_loop(0, group_b, greet_b, 0)
    pl.semaphore_wait(barrier, group_a - 1 + group_b - n_cross)

    def each_peer(p, action):
        pm = p // n_cross
        pc = p % n_cross

        @pl.when(jnp.logical_and(pc == cross, pm != mach))
        def _():
            action(p, 0, 16)

        @pl.when(jnp.logical_and(pm == mach, pc != cross))
        def _():
            action(p, 8, 16)

        @pl.when(jnp.logical_and(pm != mach, pc != cross))
        def _():
            action(p, 8, 8)

    def start_a(p, lo, size):
        pltpu.make_async_remote_copy(
            src_ref=pay_ref.at[pl.ds(lo, size)], dst_ref=recv_a.at[me_a, pl.ds(lo, size)],
            send_sem=send_a.at[p], recv_sem=got_a.at[me_a], device_id=peer_a(p), device_id_type=MESH,
        ).start()

    def finish_a(p, lo, size):
        pltpu.make_async_remote_copy(
            src_ref=pay_ref.at[pl.ds(lo, size)], dst_ref=recv_a.at[p, pl.ds(lo, size)],
            send_sem=send_a.at[p], recv_sem=got_a.at[p], device_id=peer_a(p), device_id_type=MESH,
        ).wait()

    def send_loop_a(p, carry):
        each_peer(p, start_a)
        return carry

    def wait_loop_a(p, carry):
        each_peer(p, finish_a)
        return carry

    lax.fori_loop(0, group_a, send_loop_a, 0)
    recv_a[me_a] = pay_ref[...]
    lax.fori_loop(0, group_a, wait_loop_a, 0)

    terms = recv_a[0, 8:16, :]
    for p in range(1, group_a):
        terms = terms + recv_a[p, 8:16, :]
    gm = recv_a[cross, 0:8, :]
    for q in range(1, n_mach):
        gm = gm + recv_a[q * n_cross + cross, 0:8, :]
    gc = recv_a[mach * n_cross, 16:24, :]
    for q in range(1, n_cross):
        gc = gc + recv_a[mach * n_cross + q, 16:24, :]
    for g in range(4):
        lanes = slice(g * 32, (g + 1) * 32)
        gm_s[pl.ds(g, 8, stride=4), :] = gm[:, lanes]
        mt_s[pl.ds(g, 8, stride=4), :] = terms[:, lanes]
        gc_s[pl.ds(g, 8, stride=4), :] = gc[:, lanes]

    gram = gm_s[...] * gc_s[...]
    target = mt_s[...]
    rf_ref[...] = start_ref[...]
    for r in range(rank):
        rows = rf_ref[...]
        mixed = jnp.sum(gram[:, r : r + 1] * rows, axis=0, keepdims=True)
        current = rows[r : r + 1, :]
        updated = jnp.maximum(current + (target[r : r + 1, :] - mixed) / gram[r : r + 1, r : r + 1], 0.0)
        rf_ref[r : r + 1, :] = updated

    factor = rf_ref[...]
    term = part_ref[0] * factor[:, 0:1]
    for i in range(1, part_ref.shape[0]):
        term = term + part_ref[i] * factor[:, i : i + 1]
    term_s[...] = term
    span = term_s.shape[1] // n_cross
    per_row = 128 // span
    for c in range(n_cross):
        for r in range(rank):
            pieces[c, r // per_row : r // per_row + 1, (r % per_row) * span : (r % per_row + 1) * span] = (
                term_s[r : r + 1, c * span : (c + 1) * span])

    def send_loop_b(p, carry):
        @pl.when(p != me_b)
        def _():
            pltpu.make_async_remote_copy(
                src_ref=pieces.at[p % n_cross], dst_ref=recv_b.at[me_b],
                send_sem=send_b.at[p], recv_sem=got_b.at[me_b], device_id=peer_b(p), device_id_type=MESH,
            ).start()
        return carry

    def wait_loop_b(p, carry):
        @pl.when(p != me_b)
        def _():
            pltpu.make_async_remote_copy(
                src_ref=pieces.at[p % n_cross], dst_ref=recv_b.at[p],
                send_sem=send_b.at[p], recv_sem=got_b.at[p], device_id=peer_b(p), device_id_type=MESH,
            ).wait()
        return carry

    lax.fori_loop(0, group_b, send_loop_b, 0)
    recv_b[me_b] = pieces[cross]
    lax.fori_loop(0, group_b, wait_loop_b, 0)

    total = recv_b[0]
    for p in range(1, group_b):
        total = total + recv_b[p]
    total_s[...] = total * scale
    for r in range(rank):
        mode_ref[r : r + 1, :] = total_s[r // per_row : r // per_row + 1, (r % per_row) * span : (r % per_row + 1) * span]


def local(density, roll_start, mach_factor, cross_factor):
    rolls_here, bins_here, cross_here = density.shape
    rank = cross_factor.shape[0]
    n_roll = lax.axis_size("roll")
    n_mach = lax.axis_size("mach")
    n_cross = lax.axis_size("cross")
    flat = density.reshape(rolls_here * bins_here, cross_here)
    partial_value = lax.dot_general(
        cross_factor, flat, (((1,), (1,)), ((), ())), preferred_element_type=jnp.float32
    )
    partial_value = partial_value.reshape(rank, rolls_here, bins_here)
    local_terms = jnp.einsum(
        "rij,rj->ri", partial_value, mach_factor.astype(jnp.float32), precision=lax.Precision.HIGHEST
    )
    local_mach = jnp.dot(mach_factor, mach_factor.T, preferred_element_type=jnp.float32)
    local_cross = jnp.dot(cross_factor, cross_factor.T, preferred_element_type=jnp.float32)
    pay = jnp.stack([local_mach, local_terms, local_cross]).reshape(3 * rank * rank // 128, 128)

    span = bins_here // n_cross
    scale = rank / (rolls_here * n_roll * cross_here * n_cross)
    roll_factor, mode_two = pl.pallas_call(
        functools.partial(fused_kernel, n_roll, n_cross, scale),
        out_shape=(
            jax.ShapeDtypeStruct(roll_start.shape, jnp.float32),
            jax.ShapeDtypeStruct((rank, span), jnp.float32),
        ),
        in_specs=[pl.BlockSpec(memory_space=VMEM)] * 3,
        out_specs=[pl.BlockSpec(memory_space=VMEM)] * 2,
        scratch_shapes=[
            VMEM((n_mach * n_cross,) + pay.shape, jnp.float32),
            pltpu.SemaphoreType.DMA((n_mach * n_cross,)),
            pltpu.SemaphoreType.DMA((n_mach * n_cross,)),
            VMEM((rank, rank), jnp.float32),
            VMEM((rank, rank), jnp.float32),
            VMEM((rank, rank), jnp.float32),
            VMEM((rank, bins_here), jnp.float32),
            VMEM((n_cross, rank * span // 128, 128), jnp.float32),
            VMEM((n_roll * n_cross, rank * span // 128, 128), jnp.float32),
            pltpu.SemaphoreType.DMA((n_roll * n_cross,)),
            pltpu.SemaphoreType.DMA((n_roll * n_cross,)),
            VMEM((rank * span // 128, 128), jnp.float32),
        ],
        compiler_params=pltpu.CompilerParams(collective_id=0, has_side_effects=True),
    )(pay, partial_value.transpose(1, 0, 2), roll_start)
    return (roll_factor, mode_two)


def solution(mesh):
    in_specs = (P("roll", "mach", "cross"), P(None, "roll"), P(None, "mach"), P(None, "cross"))
    out_specs = (P(None, "roll"), P(None, ("mach", "cross")))
    return jax.shard_map(local, mesh=mesh, in_specs=in_specs, out_specs=out_specs, check_vma=False)
```

time: 585 us -> 44 us (0.08)
  the two profiles are of different devices: /device:TPU:1 before, /device:TPU:63 now
where the time goes in v3:
time: 44 us; the launch traced here: 43.6 us
  Pallas kernels  31.5 us (72%)
  matrix products  8.16 us (19%)
  local copies, waits for them, and re-layouts  3.36 us (8%)
  between operations  0.67 us (2%)
    pallas_call x1, Pallas kernels, local(): pl.pallas_call(functools.partial(fused_kernel, n_roll, n_cross, scale), o...  31.5 us
    dot_general x1, matrix products, local(): lax.dot_general(cross_factor, flat, (((1,), (1,)), ((), ())), preferred_e...  5.92 us
    unnamed x8, local copies, waits for them, and re-layouts  2.68 us
    dot_general x1, matrix products, local(): jnp.einsum('rij,rj->ri', partial_value, mach_factor.astype(jnp.float32),...  1.18 us
    dot_general x1, matrix products, local(): jnp.dot(mach_factor, mach_factor.T, preferred_element_type=jnp.float32)  0.94 us

profile of v3, /device:TPU:63, one launch (start us, length us, event | category | flops | bytes accessed | tf_op | source)
XLA Modules:
  0.0 43.6 jit_solution(13780275295248233280)
XLA Ops:
  0.6 0.0 copy-start
  0.6 0.0 copy-start.2
  0.7 0.9 %convolution_bitcast_fusion.1 = f32[1,32,32]{2,1,0:T(8,128)S(1)} fusion(bf16[32,256]{1,0:T(8,128)(2,1)} %param.6), kind=kOutput, calls=%fused_computation.1 | convolution fusion | flops 524288 | bytes 20480 | tf_op jit(solution)/shard_map/dot_general | solution.py:171
  1.6 0.0 copy-done
  1.6 0.1 convolution_bitcast_fusion
  1.7 5.9 %fusion.2 = f32[32,32,256]{2,0,1:T(8,128)S(1)} fusion(bf16[32,256,512]{2,1,0:T(8,128)(2,1)} %param.4, bf16[32,512]{1,0:T(8,128)(2,1)S(1)} %copy-done), kind=kOutput, calls=%fused_computation.5 | convolution fusion | flops 268435456 | bytes 9469952 | tf_op jit(solution)/shard_map/dot_general | solution.py:164
  7.6 0.0 copy-start.1
  7.6 0.0 copy-done.2
  7.7 1.2 %fusion = f32[32,1,32]{2,1,0:T(1,128)S(1)} fusion(f32[32,32,256]{2,0,1:T(8,128)S(1)} %fusion.2, bf16[32,256,1]{1,0,2:T(8,128)(2,1)S(1)} %bitcast.18), kind=kOutput, calls=%fused_computation.2 | convolution fusion | flops 3145728 | bytes 1069056 | tf_op jit(solution)/shard_map/rij,rj->ri/dot_general | solution.py:168
  8.9 0.7 %reshape.11.pay_ref = f32[24,128]{1,0:T(8,128)} reshape(f32[3,32,32]{2,1,0:T(8,128)S(1)} %pad_maximum_fusion) | data formatting | bytes 24576 | tf_op jit(solution)/shard_map/reshape | solution.py:173
  9.5 0.0 copy-done.1
  9.5 31.5 %shard_map.59 = (f32[32,32]{1,0:T(8,128)}, f32[32,64]{1,0:T(8,128)}) custom-call(f32[24,128]{1,0:T(8,128)} %reshape.11.pay_ref, f32[32,32,256]{2,1,0:T(8,128)} %bitcast.17, f32[32,32]{1,0:T(8,128)} %start_ref.1), custom_call_target="tpu_custom_call" | custom-call | tf_op jit(solution)/shard_map/pallas_call | solution.py:177
  41.0 1.3 %copy.15 = f32[32,32]{1,0:T(8,128)} copy(f32[32,32]{1,0:T(8,128)} %get-tuple-element.4) | data formatting | bytes 8192
  42.3 1.3 %copy.16 = f32[32,64]{1,0:T(8,128)} copy(f32[32,64]{1,0:T(8,128)} %get-tuple-element.5) | data formatting | bytes 16384
  (1 shorter events, 0.0 us)
Async XLA Ops:
  0.6 1.0 %copy-start = (bf16[32,512]{1,0:T(8,128)(2,1)S(1)}, bf16[32,512]{1,0:T(8,128)(2,1)}, u32[]{:S(2)}) copy-start(bf16[32,512]{1,0:T(8,128)(2,1)} %param.7) | copy-start | bytes 98308
  0.6 7.0 %copy-start.2 = (bf16[32,256]{1,0:T(8,128)(2,1)S(1)}, bf16[32,256]{1,0:T(8,128)(2,1)}, u32[]{:S(2)}) copy-start(bf16[32,256]{1,0:T(8,128)(2,1)} %param.6) | copy-start | bytes 49156
  7.6 1.9 %copy-start.1 = (f32[32,32,256]{2,0,1:T(8,128)}, f32[32,32,256]{2,0,1:T(8,128)S(1)}, u32[]{:S(2)}) copy-start(f32[32,32,256]{2,0,1:T(8,128)S(1)} %fusion.2) | copy-start | bytes 3145732

commit v4 on v3

--- a/solution.py
+++ b/solution.py
@@ -11,7 +11,8 @@
 VMEM = pltpu.VMEM
 
 
-def fused_kernel(n_roll, n_cross, scale, pay_ref, part_ref, start_ref, rf_ref, mode_ref,
+def fused_kernel(n_roll, n_cross, scale, n_chunks, dens_hbm, cross_ref, mach_ref, start_ref, rf_ref, mode_ref,
+                 dens_v, dens_sem, part_ref, local_s, pay_ref,
                  recv_a, send_a, got_a, gm_s, mt_s, gc_s, term_s, pieces, recv_b, send_b, got_b, total_s):
     roll = lax.axis_index("roll")
     mach = lax.axis_index("mach")
@@ -29,6 +30,15 @@
     def peer_b(p):
         return (p // n_cross, mach, p % n_cross)
 
+    rolls_here = dens_v.shape[0]
+    chunk = rolls_here // n_chunks
+    loads = [
+        pltpu.make_async_copy(dens_hbm.at[pl.ds(k * chunk, chunk)], dens_v.at[pl.ds(k * chunk, chunk)], dens_sem.at[k])
+        for k in range(n_chunks)
+    ]
+    for load in loads:
+        load.start()
+
     barrier = pltpu.get_barrier_semaphore()
 
     def greet_a(p, carry):
@@ -45,6 +55,27 @@
 
     lax.fori_loop(0, group_a, greet_a, 0)
     lax.fori_loop(0, group_b, greet_b, 0)
+
+    nt = (((1,), (1,)), ((), ()))
+    cross_f = cross_ref[...]
+    mach_f = mach_ref[...]
+    mach_w = mach_f.astype(jnp.float32)
+    local_s[0] = lax.dot_general(mach_f, mach_f, nt, preferred_element_type=jnp.float32)
+    local_s[2] = lax.dot_general(cross_f, cross_f, nt, preferred_element_type=jnp.float32)
+    lane = lax.broadcasted_iota(jnp.int32, (rank, rolls_here), 1)
+    terms_local = jnp.zeros((rank, rolls_here), jnp.float32)
+    for k in range(n_chunks):
+        loads[k].wait()
+        for i in range(k * chunk, (k + 1) * chunk):
+            value = lax.dot_general(cross_f, dens_v[i], nt, preferred_element_type=jnp.float32)
+            part_ref[i] = value
+            column = jnp.sum(value * mach_w, axis=1, keepdims=True)
+            terms_local = jnp.where(lane == i, column, terms_local)
+    local_s[1] = terms_local
+    for k in range(3):
+        for g in range(4):
+            pay_ref[8 * k : 8 * k + 8, g * 32 : (g + 1) * 32] = local_s[k, pl.ds(g, 8, stride=4), :]
+
     pl.semaphore_wait(barrier, group_a - 1 + group_b - n_cross)
 
     def each_peer(p, action):
@@ -160,30 +191,25 @@
     n_roll = lax.axis_size("roll")
     n_mach = lax.axis_size("mach")
     n_cross = lax.axis_size("cross")
-    flat = density.reshape(rolls_here * bins_here, cross_here)
-    partial_value = lax.dot_general(
-        cross_factor, flat, (((1,), (1,)), ((), ())), preferred_element_type=jnp.float32
-    )
-    partial_value = partial_value.reshape(rank, rolls_here, bins_here)
-    local_terms = jnp.einsum(
-        "rij,rj->ri", partial_value, mach_factor.astype(jnp.float32), precision=lax.Precision.HIGHEST
-    )
-    local_mach = jnp.dot(mach_factor, mach_factor.T, preferred_element_type=jnp.float32)
-    local_cross = jnp.dot(cross_factor, cross_factor.T, preferred_element_type=jnp.float32)
-    pay = jnp.stack([local_mach, local_terms, local_cross]).reshape(3 * rank * rank // 128, 128)
-
+    n_chunks = 4
+    pay_rows = 3 * rank * rank // 128
     span = bins_here // n_cross
     scale = rank / (rolls_here * n_roll * cross_here * n_cross)
     roll_factor, mode_two = pl.pallas_call(
-        functools.partial(fused_kernel, n_roll, n_cross, scale),
+        functools.partial(fused_kernel, n_roll, n_cross, scale, n_chunks),
         out_shape=(
             jax.ShapeDtypeStruct(roll_start.shape, jnp.float32),
             jax.ShapeDtypeStruct((rank, span), jnp.float32),
         ),
-        in_specs=[pl.BlockSpec(memory_space=VMEM)] * 3,
+        in_specs=[pl.BlockSpec(memory_space=pl.ANY)] + [pl.BlockSpec(memory_space=VMEM)] * 3,
         out_specs=[pl.BlockSpec(memory_space=VMEM)] * 2,
         scratch_shapes=[
-            VMEM((n_mach * n_cross,) + pay.shape, jnp.float32),
+            VMEM(density.shape, density.dtype),
+            pltpu.SemaphoreType.DMA((n_chunks,)),
+            VMEM((rolls_here, rank, bins_here), jnp.float32),
+            VMEM((3, rank, rank), jnp.float32),
+            VMEM((pay_rows, 128), jnp.float32),
+            VMEM((n_mach * n_cross, pay_rows, 128), jnp.float32),
             pltpu.SemaphoreType.DMA((n_mach * n_cross,)),
             pltpu.SemaphoreType.DMA((n_mach * n_cross,)),
             VMEM((rank, rank), jnp.float32),
@@ -197,7 +223,7 @@
             VMEM((rank * span // 128, 128), jnp.float32),
         ],
         compiler_params=pltpu.CompilerParams(collective_id=0, has_side_effects=True),
-    )(pay, partial_value.transpose(1, 0, 2), roll_start)
+    )(density, cross_factor, mach_factor, roll_start)
     return (roll_factor, mode_two)
 
 

time: 44 us -> 35 us (0.80)
  the two profiles are of different devices: /device:TPU:63 before, /device:TPU:25 now
where the time goes in v4:
time: 35 us; the launch traced here: 34.6 us
  Pallas kernels  31.3 us (89%)
  local copies, waits for them, and re-layouts  2.65 us (8%)
  between operations  0.64 us (2%)
    pallas_call x1, Pallas kernels, local(): pl.pallas_call(functools.partial(fused_kernel, n_roll, n_cross, scale, n_...  31.3 us
    unnamed x2, local copies, waits for them, and re-layouts  2.65 us

profile of v4, /device:TPU:25, one launch (start us, length us, event | category | flops | bytes accessed | tf_op | source)
XLA Modules:
  0.0 34.6 jit_solution(419538949919883274)
XLA Ops:
  0.6 31.3 %shard_map.59 = (f32[32,32]{1,0:T(8,128)}, f32[32,64]{1,0:T(8,128)}) custom-call(bf16[32,256,512]{2,1,0:T(8,128)(2,1)} %dens_hbm.1, bf16[32,512]{1,0:T(8,128)(2,1)} %cross_ref.1, bf16[32,256]{1,0:T(8,128)(2,1)} %mach_ref.1, f32[32,32]{1,0:T(8,128)} %start_ref.1), custom_call_target="tpu_custom_call" | custom-call | tf_op jit(solution)/shard_map/pallas_call | solution.py:198
  32.0 1.3 %copy.8 = f32[32,32]{1,0:T(8,128)} copy(f32[32,32]{1,0:T(8,128)} %get-tuple-element.4) | data formatting | bytes 8192
  33.3 1.3 %copy.9 = f32[32,64]{1,0:T(8,128)} copy(f32[32,64]{1,0:T(8,128)} %get-tuple-element.5) | data formatting | bytes 16384

commit v5 on v4

--- a/solution.py
+++ b/solution.py
@@ -135,13 +135,15 @@
 
     gram = gm_s[...] * gc_s[...]
     target = mt_s[...]
-    rf_ref[...] = start_ref[...]
+    rows = start_ref[...]
+    mixed = gram[:, 0:1] * rows[0:1, :]
+    for s_ in range(1, rank):
+        mixed = mixed + gram[:, s_ : s_ + 1] * rows[s_ : s_ + 1, :]
     for r in range(rank):
-        rows = rf_ref[...]
-        mixed = jnp.sum(gram[:, r : r + 1] * rows, axis=0, keepdims=True)
         current = rows[r : r + 1, :]
-        updated = jnp.maximum(current + (target[r : r + 1, :] - mixed) / gram[r : r + 1, r : r + 1], 0.0)
+        updated = jnp.maximum(current + (target[r : r + 1, :] - mixed[r : r + 1, :]) / gram[r : r + 1, r : r + 1], 0.0)
         rf_ref[r : r + 1, :] = updated
+        mixed = mixed + gram[:, r : r + 1] * (updated - current)
 
     factor = rf_ref[...]
     term = part_ref[0] * factor[:, 0:1]

time: 35 us -> 34.8 us (level)
  no operation moved by 1% of the time
where the time goes in v5:
time: 34.8 us; the launch traced here: 34.4 us
  Pallas kernels  31.1 us (89%)
  local copies, waits for them, and re-layouts  2.65 us (8%)
  between operations  0.64 us (2%)
    pallas_call x1, Pallas kernels, local(): pl.pallas_call(functools.partial(fused_kernel, n_roll, n_cross, scale, n_...  31.1 us
    unnamed x2, local copies, waits for them, and re-layouts  2.65 us

profile of v5, /device:TPU:25, one launch (start us, length us, event | category | flops | bytes accessed | tf_op | source)
XLA Modules:
  0.0 34.4 jit_solution(15494355365820144344)
XLA Ops:
  0.6 31.1 %shard_map.59 = (f32[32,32]{1,0:T(8,128)}, f32[32,64]{1,0:T(8,128)}) custom-call(bf16[32,256,512]{2,1,0:T(8,128)(2,1)} %dens_hbm.1, bf16[32,512]{1,0:T(8,128)(2,1)} %cross_ref.1, bf16[32,256]{1,0:T(8,128)(2,1)} %mach_ref.1, f32[32,32]{1,0:T(8,128)} %start_ref.1), custom_call_target="tpu_custom_call" | custom-call | tf_op jit(solution)/shard_map/pallas_call | solution.py:200
  31.7 1.3 %copy.8 = f32[32,32]{1,0:T(8,128)} copy(f32[32,32]{1,0:T(8,128)} %get-tuple-element.4) | data formatting | bytes 8192
  33.1 1.3 %copy.9 = f32[32,64]{1,0:T(8,128)} copy(f32[32,64]{1,0:T(8,128)} %get-tuple-element.5) | data formatting | bytes 16384

commit v6 on v5

--- a/solution.py
+++ b/solution.py
@@ -62,8 +62,42 @@
     mach_w = mach_f.astype(jnp.float32)
     local_s[0] = lax.dot_general(mach_f, mach_f, nt, preferred_element_type=jnp.float32)
     local_s[2] = lax.dot_general(cross_f, cross_f, nt, preferred_element_type=jnp.float32)
+    for k in (0, 2):
+        for g in range(4):
+            pay_ref[8 * k : 8 * k + 8, g * 32 : (g + 1) * 32] = local_s[k, pl.ds(g, 8, stride=4), :]
+
+    def start_rows(p, lo, size):
+        pltpu.make_async_remote_copy(
+            src_ref=pay_ref.at[pl.ds(lo, size)], dst_ref=recv_a.at[me_a, pl.ds(lo, size)],
+            send_sem=send_a.at[p], recv_sem=got_a.at[me_a], device_id=peer_a(p), device_id_type=MESH,
+        ).start()
+
+    def send_grams(p, carry):
+        pm = p // n_cross
+        pc = p % n_cross
+
+        @pl.when(jnp.logical_and(pc == cross, pm != mach))
+        def _():
+            start_rows(p, 0, 8)
+
+        @pl.when(jnp.logical_and(pm == mach, pc != cross))
+        def _():
+            start_rows(p, 16, 8)
+        return carry
+
+    chunk_rows = chunk * rank // 128
+
+    def send_chunk(k):
+        def body(p, carry):
+            @pl.when(p != me_a)
+            def _():
+                start_rows(p, 8 + k * chunk_rows, chunk_rows)
+            return carry
+        lax.fori_loop(0, group_a, body, 0)
+
     lane = lax.broadcasted_iota(jnp.int32, (rank, rolls_here), 1)
     terms_local = jnp.zeros((rank, rolls_here), jnp.float32)
+    wait_after = max(n_chunks - 2, 0)
     for k in range(n_chunks):
         loads[k].wait()
         for i in range(k * chunk, (k + 1) * chunk):
@@ -71,12 +105,18 @@
             part_ref[i] = value
             column = jnp.sum(value * mach_w, axis=1, keepdims=True)
             terms_local = jnp.where(lane == i, column, terms_local)
-    local_s[1] = terms_local
-    for k in range(3):
-        for g in range(4):
-            pay_ref[8 * k : 8 * k + 8, g * 32 : (g + 1) * 32] = local_s[k, pl.ds(g, 8, stride=4), :]
-
-    pl.semaphore_wait(barrier, group_a - 1 + group_b - n_cross)
+        local_s[1] = terms_local.T
+        for h in range(chunk_rows):
+            for g in range(4):
+                pay_ref[8 + k * chunk_rows + h : 9 + k * chunk_rows + h, g * 32 : (g + 1) * 32] = (
+                    local_s[1, k * chunk + 4 * h + g : k * chunk + 4 * h + g + 1, :])
+        if k == wait_after:
+            pl.semaphore_wait(barrier, group_a - 1 + group_b - n_cross)
+            lax.fori_loop(0, group_a, send_grams, 0)
+            for c in range(k + 1):
+                send_chunk(c)
+        elif k > wait_after:
+            send_chunk(k)
 
     def each_peer(p, action):
         pm = p // n_cross
@@ -93,12 +133,6 @@
         @pl.when(jnp.logical_and(pm != mach, pc != cross))
         def _():
             action(p, 8, 8)
-
-    def start_a(p, lo, size):
-        pltpu.make_async_remote_copy(
-            src_ref=pay_ref.at[pl.ds(lo, size)], dst_ref=recv_a.at[me_a, pl.ds(lo, size)],
-            send_sem=send_a.at[p], recv_sem=got_a.at[me_a], device_id=peer_a(p), device_id_type=MESH,
-        ).start()
 
     def finish_a(p, lo, size):
         pltpu.make_async_remote_copy(
@@ -106,15 +140,10 @@
             send_sem=send_a.at[p], recv_sem=got_a.at[p], device_id=peer_a(p), device_id_type=MESH,
         ).wait()
 
-    def send_loop_a(p, carry):
-        each_peer(p, start_a)
-        return carry
-
     def wait_loop_a(p, carry):
         each_peer(p, finish_a)
         return carry
 
-    lax.fori_loop(0, group_a, send_loop_a, 0)
     recv_a[me_a] = pay_ref[...]
     lax.fori_loop(0, group_a, wait_loop_a, 0)
 
@@ -134,7 +163,7 @@
         gc_s[pl.ds(g, 8, stride=4), :] = gc[:, lanes]
 
     gram = gm_s[...] * gc_s[...]
-    target = mt_s[...]
+    target = mt_s[...].T
     rows = start_ref[...]
     mixed = gram[:, 0:1] * rows[0:1, :]
     for s_ in range(1, rank):

time: 34.8 us -> 37.3 us (1.072)
  the two profiles are of different devices: /device:TPU:25 before, /device:TPU:1 now
where the time goes in v6:
time: 37.3 us; the launch traced here: 36.9 us
  Pallas kernels  33.6 us (90%)
  local copies, waits for them, and re-layouts  2.65 us (7%)
  between operations  0.64 us (2%)
    pallas_call x1, Pallas kernels, local(): pl.pallas_call(functools.partial(fused_kernel, n_roll, n_cross, scale, n_...  33.6 us
    unnamed x2, local copies, waits for them, and re-layouts  2.65 us

profile of v6, /device:TPU:1, one launch (start us, length us, event | category | flops | bytes accessed | tf_op | source)
XLA Modules:
  0.0 36.9 jit_solution(17884071026798050091)
XLA Ops:
  0.6 33.6 %shard_map.59 = (f32[32,32]{1,0:T(8,128)}, f32[32,64]{1,0:T(8,128)}) custom-call(bf16[32,256,512]{2,1,0:T(8,128)(2,1)} %dens_hbm.1, bf16[32,512]{1,0:T(8,128)(2,1)} %cross_ref.1, bf16[32,256]{1,0:T(8,128)(2,1)} %mach_ref.1, f32[32,32]{1,0:T(8,128)} %start_ref.1), custom_call_target="tpu_custom_call" | custom-call | tf_op jit(solution)/shard_map/pallas_call | solution.py:229
  34.2 1.3 %copy.8 = f32[32,32]{1,0:T(8,128)} copy(f32[32,32]{1,0:T(8,128)} %get-tuple-element.4) | data formatting | bytes 8192
  35.5 1.3 %copy.9 = f32[32,64]{1,0:T(8,128)} copy(f32[32,64]{1,0:T(8,128)} %get-tuple-element.5) | data formatting | bytes 16384

commit v7 on v5

--- a/solution.py
+++ b/solution.py
@@ -13,19 +13,20 @@
 
 def fused_kernel(n_roll, n_cross, scale, n_chunks, dens_hbm, cross_ref, mach_ref, start_ref, rf_ref, mode_ref,
                  dens_v, dens_sem, part_ref, local_s, pay_ref,
-                 recv_a, send_a, got_a, gm_s, mt_s, gc_s, term_s, pieces, recv_b, send_b, got_b, total_s):
+                 recv_1, send_1, got_1, pay_2, recv_2, send_2, got_2, gm_s, mt_s, gc_s, term_s, pieces, recv_b, send_b, got_b, total_s):
     roll = lax.axis_index("roll")
     mach = lax.axis_index("mach")
     cross = lax.axis_index("cross")
-    group_a = recv_a.shape[0]
+    n_mach = recv_2.shape[0]
     group_b = recv_b.shape[0]
-    n_mach = group_a // n_cross
-    me_a = mach * n_cross + cross
     me_b = roll * n_cross + cross
     rank = rf_ref.shape[0]
 
-    def peer_a(p):
-        return (roll, p // n_cross, p % n_cross)
+    def peer_c(p):
+        return (roll, mach, p)
+
+    def peer_m(p):
+        return (roll, p, cross)
 
     def peer_b(p):
         return (p // n_cross, mach, p % n_cross)
@@ -41,10 +42,10 @@
 
     barrier = pltpu.get_barrier_semaphore()
 
-    def greet_a(p, carry):
-        @pl.when(p != me_a)
-        def _():
-            pl.semaphore_signal(barrier, inc=1, device_id=peer_a(p), device_id_type=MESH)
+    def greet_m(p, carry):
+        @pl.when(p != mach)
+        def _():
+            pl.semaphore_signal(barrier, inc=1, device_id=peer_m(p), device_id_type=MESH)
         return carry
 
     def greet_b(p, carry):
@@ -53,7 +54,11 @@
             pl.semaphore_signal(barrier, inc=1, device_id=peer_b(p), device_id_type=MESH)
         return carry
 
-    lax.fori_loop(0, group_a, greet_a, 0)
+    lax.fori_loop(0, n_mach, greet_m, 0)
+    for p in range(n_cross):
+        @pl.when(p != cross)
+        def _():
+            pl.semaphore_signal(barrier, inc=1, device_id=peer_c(p), device_id_type=MESH)
     lax.fori_loop(0, group_b, greet_b, 0)
 
     nt = (((1,), (1,)), ((), ()))
@@ -76,57 +81,60 @@
         for g in range(4):
             pay_ref[8 * k : 8 * k + 8, g * 32 : (g + 1) * 32] = local_s[k, pl.ds(g, 8, stride=4), :]
 
-    pl.semaphore_wait(barrier, group_a - 1 + group_b - n_cross)
-
-    def each_peer(p, action):
-        pm = p // n_cross
-        pc = p % n_cross
-
-        @pl.when(jnp.logical_and(pc == cross, pm != mach))
-        def _():
-            action(p, 0, 16)
-
-        @pl.when(jnp.logical_and(pm == mach, pc != cross))
-        def _():
-            action(p, 8, 16)
-
-        @pl.when(jnp.logical_and(pm != mach, pc != cross))
-        def _():
-            action(p, 8, 8)
-
-    def start_a(p, lo, size):
-        pltpu.make_async_remote_copy(
-            src_ref=pay_ref.at[pl.ds(lo, size)], dst_ref=recv_a.at[me_a, pl.ds(lo, size)],
-            send_sem=send_a.at[p], recv_sem=got_a.at[me_a], device_id=peer_a(p), device_id_type=MESH,
-        ).start()
-
-    def finish_a(p, lo, size):
-        pltpu.make_async_remote_copy(
-            src_ref=pay_ref.at[pl.ds(lo, size)], dst_ref=recv_a.at[p, pl.ds(lo, size)],
-            send_sem=send_a.at[p], recv_sem=got_a.at[p], device_id=peer_a(p), device_id_type=MESH,
-        ).wait()
-
-    def send_loop_a(p, carry):
-        each_peer(p, start_a)
-        return carry
-
-    def wait_loop_a(p, carry):
-        each_peer(p, finish_a)
-        return carry
-
-    lax.fori_loop(0, group_a, send_loop_a, 0)
-    recv_a[me_a] = pay_ref[...]
-    lax.fori_loop(0, group_a, wait_loop_a, 0)
-
-    terms = recv_a[0, 8:16, :]
-    for p in range(1, group_a):
-        terms = terms + recv_a[p, 8:16, :]
-    gm = recv_a[cross, 0:8, :]
-    for q in range(1, n_mach):
-        gm = gm + recv_a[q * n_cross + cross, 0:8, :]
-    gc = recv_a[mach * n_cross, 16:24, :]
-    for q in range(1, n_cross):
-        gc = gc + recv_a[mach * n_cross + q, 16:24, :]
+    pl.semaphore_wait(barrier, n_mach - 1 + group_b - 1)
+
+    def stage_1(p):
+        return pltpu.make_async_remote_copy(
+            src_ref=pay_ref.at[pl.ds(8, 16)], dst_ref=recv_1.at[cross], send_sem=send_1.at[p],
+            recv_sem=got_1.at[cross], device_id=peer_c(p), device_id_type=MESH)
+
+    def stage_1_in(p):
+        return pltpu.make_async_remote_copy(
+            src_ref=pay_ref.at[pl.ds(8, 16)], dst_ref=recv_1.at[p], send_sem=send_1.at[p],
+            recv_sem=got_1.at[p], device_id=peer_c(p), device_id_type=MESH)
+
+    for p in range(n_cross):
+        @pl.when(p != cross)
+        def _():
+            stage_1(p).start()
+    recv_1[cross] = pay_ref[8:24, :]
+    for p in range(n_cross):
+        @pl.when(p != cross)
+        def _():
+            stage_1_in(p).wait()
+    terms = recv_1[0, 0:8, :]
+    gc = recv_1[0, 8:16, :]
+    for p in range(1, n_cross):
+        terms = terms + recv_1[p, 0:8, :]
+        gc = gc + recv_1[p, 8:16, :]
+
+    pay_2[0:8, :] = pay_ref[0:8, :]
+    pay_2[8:16, :] = terms
+
+    def send_loop_2(p, carry):
+        @pl.when(p != mach)
+        def _():
+            pltpu.make_async_remote_copy(
+                src_ref=pay_2, dst_ref=recv_2.at[mach], send_sem=send_2.at[p], recv_sem=got_2.at[mach],
+                device_id=peer_m(p), device_id_type=MESH).start()
+        return carry
+
+    def wait_loop_2(p, carry):
+        @pl.when(p != mach)
+        def _():
+            pltpu.make_async_remote_copy(
+                src_ref=pay_2, dst_ref=recv_2.at[p], send_sem=send_2.at[p], recv_sem=got_2.at[p],
+                device_id=peer_m(p), device_id_type=MESH).wait()
+        return carry
+
+    lax.fori_loop(0, n_mach, send_loop_2, 0)
+    recv_2[mach] = pay_2[...]
+    lax.fori_loop(0, n_mach, wait_loop_2, 0)
+    gm = recv_2[0, 0:8, :]
+    terms = recv_2[0, 8:16, :]
+    for p in range(1, n_mach):
+        gm = gm + recv_2[p, 0:8, :]
+        terms = terms + recv_2[p, 8:16, :]
     for g in range(4):
         lanes = slice(g * 32, (g + 1) * 32)
         gm_s[pl.ds(g, 8, stride=4), :] = gm[:, lanes]
@@ -211,9 +219,13 @@
             VMEM((rolls_here, rank, bins_here), jnp.float32),
             VMEM((3, rank, rank), jnp.float32),
             VMEM((pay_rows, 128), jnp.float32),
-            VMEM((n_mach * n_cross, pay_rows, 128), jnp.float32),
-            pltpu.SemaphoreType.DMA((n_mach * n_cross,)),
-            pltpu.SemaphoreType.DMA((n_mach * n_cross,)),
+            VMEM((n_cross, 16, 128), jnp.float32),
+            pltpu.SemaphoreType.DMA((n_cross,)),
+            pltpu.SemaphoreType.DMA((n_cross,)),
+            VMEM((16, 128), jnp.float32),
+            VMEM((n_mach, 16, 128), jnp.float32),
+            pltpu.SemaphoreType.DMA((n_mach,)),
+            pltpu.SemaphoreType.DMA((n_mach,)),
             VMEM((rank, rank), jnp.float32),
             VMEM((rank, rank), jnp.float32),
             VMEM((rank, rank), jnp.float32),

time: 34.8 us -> 32.6 us (0.937)
  the two profiles are of different devices: /device:TPU:25 before, /device:TPU:1 now
where the time goes in v7:
time: 32.6 us; the launch traced here: 32.1 us
  Pallas kernels  28.9 us (89%)
  local copies, waits for them, and re-layouts  2.65 us (8%)
  between operations  0.64 us (2%)
    pallas_call x1, Pallas kernels, local(): pl.pallas_call(functools.partial(fused_kernel, n_roll, n_cross, scale, n_...  28.9 us
    unnamed x2, local copies, waits for them, and re-layouts  2.65 us

profile of v7, /device:TPU:1, one launch (start us, length us, event | category | flops | bytes accessed | tf_op | source)
XLA Modules:
  0.0 32.1 jit_solution(14984585396128474997)
XLA Ops:
  0.6 28.9 %shard_map.59 = (f32[32,32]{1,0:T(8,128)}, f32[32,64]{1,0:T(8,128)}) custom-call(bf16[32,256,512]{2,1,0:T(8,128)(2,1)} %dens_hbm.1, bf16[32,512]{1,0:T(8,128)(2,1)} %cross_ref.1, bf16[32,256]{1,0:T(8,128)(2,1)} %mach_ref.1, f32[32,32]{1,0:T(8,128)} %start_ref.1), custom_call_target="tpu_custom_call" | custom-call | tf_op jit(solution)/shard_map/pallas_call | solution.py:208
  29.5 1.3 %copy.8 = f32[32,32]{1,0:T(8,128)} copy(f32[32,32]{1,0:T(8,128)} %get-tuple-element.4) | data formatting | bytes 8192
  30.8 1.3 %copy.9 = f32[32,64]{1,0:T(8,128)} copy(f32[32,64]{1,0:T(8,128)} %get-tuple-element.5) | data formatting | bytes 16384

commit v8 on v7

--- a/solution.py
+++ b/solution.py
@@ -13,11 +13,14 @@
 
 def fused_kernel(n_roll, n_cross, scale, n_chunks, dens_hbm, cross_ref, mach_ref, start_ref, rf_ref, mode_ref,
                  dens_v, dens_sem, part_ref, local_s, pay_ref,
-                 recv_1, send_1, got_1, pay_2, recv_2, send_2, got_2, gm_s, mt_s, gc_s, term_s, pieces, recv_b, send_b, got_b, total_s):
+                 recv_1, send_1, got_1, pay_2, recv_2, send_2, got_2, pay_3, recv_3, send_3, got_3, gm_s, mt_s, gc_s, term_s, pieces, recv_b, send_b, got_b, total_s):
     roll = lax.axis_index("roll")
     mach = lax.axis_index("mach")
     cross = lax.axis_index("cross")
-    n_mach = recv_2.shape[0]
+    n_x = recv_2.shape[0]
+    n_y = recv_3.shape[0]
+    mach_y = mach // n_x
+    mach_x = mach % n_x
     group_b = recv_b.shape[0]
     me_b = roll * n_cross + cross
     rank = rf_ref.shape[0]
@@ -25,8 +28,26 @@
     def peer_c(p):
         return (roll, mach, p)
 
-    def peer_m(p):
-        return (roll, p, cross)
+    def peer_x(p):
+        return (roll, mach_y * n_x + p, cross)
+
+    def peer_y(p):
+        return (roll, p * n_x + mach_x, cross)
+
+    def exchange(src_ref, recv_ref, send_sem, recv_sem, me, peer):
+        for p in range(recv_ref.shape[0]):
+            @pl.when(p != me)
+            def _():
+                pltpu.make_async_remote_copy(
+                    src_ref=src_ref, dst_ref=recv_ref.at[me], send_sem=send_sem.at[p], recv_sem=recv_sem.at[me],
+                    device_id=peer(p), device_id_type=MESH).start()
+        recv_ref[me] = src_ref[...]
+        for p in range(recv_ref.shape[0]):
+            @pl.when(p != me)
+            def _():
+                pltpu.make_async_remote_copy(
+                    src_ref=src_ref, dst_ref=recv_ref.at[p], send_sem=send_sem.at[p], recv_sem=recv_sem.at[p],
+                    device_id=peer(p), device_id_type=MESH).wait()
 
     def peer_b(p):
         return (p // n_cross, mach, p % n_cross)
@@ -42,11 +63,6 @@
 
     barrier = pltpu.get_barrier_semaphore()
 
-    def greet_m(p, carry):
-        @pl.when(p != mach)
-        def _():
-            pl.semaphore_signal(barrier, inc=1, device_id=peer_m(p), device_id_type=MESH)
-        return carry
 
     def greet_b(p, carry):
         @pl.when(p // n_cross != roll)
@@ -54,11 +70,11 @@
             pl.semaphore_signal(barrier, inc=1, device_id=peer_b(p), device_id_type=MESH)
         return carry
 
-    lax.fori_loop(0, n_mach, greet_m, 0)
-    for p in range(n_cross):
-        @pl.when(p != cross)
-        def _():
-            pl.semaphore_signal(barrier, inc=1, device_id=peer_c(p), device_id_type=MESH)
+    for n, me, peer in ((n_cross, cross, peer_c), (n_x, mach_x, peer_x), (n_y, mach_y, peer_y)):
+        for p in range(n):
+            @pl.when(p != me)
+            def _():
+                pl.semaphore_signal(barrier, inc=1, device_id=peer(p), device_id_type=MESH)
     lax.fori_loop(0, group_b, greet_b, 0)
 
     nt = (((1,), (1,)), ((), ()))
@@ -81,7 +97,7 @@
         for g in range(4):
             pay_ref[8 * k : 8 * k + 8, g * 32 : (g + 1) * 32] = local_s[k, pl.ds(g, 8, stride=4), :]
 
-    pl.semaphore_wait(barrier, n_mach - 1 + group_b - 1)
+    pl.semaphore_wait(barrier, n_x - 1 + n_y - 1 + group_b - 1)
 
     def stage_1(p):
         return pltpu.make_async_remote_copy(
@@ -110,31 +126,20 @@
 
     pay_2[0:8, :] = pay_ref[0:8, :]
     pay_2[8:16, :] = terms
-
-    def send_loop_2(p, carry):
-        @pl.when(p != mach)
-        def _():
-            pltpu.make_async_remote_copy(
-                src_ref=pay_2, dst_ref=recv_2.at[mach], send_sem=send_2.at[p], recv_sem=got_2.at[mach],
-                device_id=peer_m(p), device_id_type=MESH).start()
-        return carry
-
-    def wait_loop_2(p, carry):
-        @pl.when(p != mach)
-        def _():
-            pltpu.make_async_remote_copy(
-                src_ref=pay_2, dst_ref=recv_2.at[p], send_sem=send_2.at[p], recv_sem=got_2.at[p],
-                device_id=peer_m(p), device_id_type=MESH).wait()
-        return carry
-
-    lax.fori_loop(0, n_mach, send_loop_2, 0)
-    recv_2[mach] = pay_2[...]
-    lax.fori_loop(0, n_mach, wait_loop_2, 0)
+    exchange(pay_2, recv_2, send_2, got_2, mach_x, peer_x)
     gm = recv_2[0, 0:8, :]
     terms = recv_2[0, 8:16, :]
-    for p in range(1, n_mach):
+    for p in range(1, n_x):
         gm = gm + recv_2[p, 0:8, :]
         terms = terms + recv_2[p, 8:16, :]
+    pay_3[0:8, :] = gm
+    pay_3[8:16, :] = terms
+    exchange(pay_3, recv_3, send_3, got_3, mach_y, peer_y)
+    gm = recv_3[0, 0:8, :]
+    terms = recv_3[0, 8:16, :]
+    for p in range(1, n_y):
+        gm = gm + recv_3[p, 0:8, :]
+        terms = terms + recv_3[p, 8:16, :]
     for g in range(4):
         lanes = slice(g * 32, (g + 1) * 32)
         gm_s[pl.ds(g, 8, stride=4), :] = gm[:, lanes]
@@ -202,6 +207,7 @@
     n_mach = lax.axis_size("mach")
     n_cross = lax.axis_size("cross")
     n_chunks = 4
+    n_x = 4 if n_mach % 4 == 0 else n_mach
     pay_rows = 3 * rank * rank // 128
     span = bins_here // n_cross
     scale = rank / (rolls_here * n_roll * cross_here * n_cross)
@@ -223,9 +229,13 @@
             pltpu.SemaphoreType.DMA((n_cross,)),
             pltpu.SemaphoreType.DMA((n_cross,)),
             VMEM((16, 128), jnp.float32),
-            VMEM((n_mach, 16, 128), jnp.float32),
-            pltpu.SemaphoreType.DMA((n_mach,)),
-            pltpu.SemaphoreType.DMA((n_mach,)),
+            VMEM((n_x, 16, 128), jnp.float32),
+            pltpu.SemaphoreType.DMA((n_x,)),
+            pltpu.SemaphoreType.DMA((n_x,)),
+            VMEM((16, 128), jnp.float32),
+            VMEM((n_mach // n_x, 16, 128), jnp.float32),
+            pltpu.SemaphoreType.DMA((n_mach // n_x,)),
+            pltpu.SemaphoreType.DMA((n_mach // n_x,)),
             VMEM((rank, rank), jnp.float32),
             VMEM((rank, rank), jnp.float32),
             VMEM((rank, rank), jnp.float32),

time: 32.6 us -> 34.6 us (1.061)
  Pallas kernels: 28.9 us -> 30.9 us
    pallas_call x1, Pallas kernels: 28.9 us -> 30.9 us  [local(): pl.pallas_call(functools.partial(fused_kernel, n_roll, n_cross, scale, n_...]
where the time goes in v8:
time: 34.6 us; the launch traced here: 34.2 us
  Pallas kernels  30.9 us (89%)
  local copies, waits for them, and re-layouts  2.65 us (8%)
  between operations  0.64 us (2%)
    pallas_call x1, Pallas kernels, local(): pl.pallas_call(functools.partial(fused_kernel, n_roll, n_cross, scale, n_...  30.9 us
    unnamed x2, local copies, waits for them, and re-layouts  2.65 us

profile of v8, /device:TPU:1, one launch (start us, length us, event | category | flops | bytes accessed | tf_op | source)
XLA Modules:
  0.0 34.2 jit_solution(13551685784750388898)
XLA Ops:
  0.6 30.9 %shard_map.59 = (f32[32,32]{1,0:T(8,128)}, f32[32,64]{1,0:T(8,128)}) custom-call(bf16[32,256,512]{2,1,0:T(8,128)(2,1)} %dens_hbm.1, bf16[32,512]{1,0:T(8,128)(2,1)} %cross_ref.1, bf16[32,256]{1,0:T(8,128)(2,1)} %mach_ref.1, f32[32,32]{1,0:T(8,128)} %start_ref.1), custom_call_target="tpu_custom_call" | custom-call | tf_op jit(solution)/shard_map/pallas_call | solution.py:214
  31.5 1.3 %copy.8 = f32[32,32]{1,0:T(8,128)} copy(f32[32,32]{1,0:T(8,128)} %get-tuple-element.4) | data formatting | bytes 8192
  32.9 1.3 %copy.9 = f32[32,64]{1,0:T(8,128)} copy(f32[32,64]{1,0:T(8,128)} %get-tuple-element.5) | data formatting | bytes 16384

commit v9 on v7

--- a/solution.py
+++ b/solution.py
@@ -13,7 +13,7 @@
 
 def fused_kernel(n_roll, n_cross, scale, n_chunks, dens_hbm, cross_ref, mach_ref, start_ref, rf_ref, mode_ref,
                  dens_v, dens_sem, part_ref, local_s, pay_ref,
-                 recv_1, send_1, got_1, pay_2, recv_2, send_2, got_2, gm_s, mt_s, gc_s, term_s, pieces, recv_b, send_b, got_b, total_s):
+                 recv_1, send_1, got_1, pay_2, recv_2, send_2, got_2, gm_s, mt_s, gc_s, term_s, pieces, recv_b, send_b, got_b):
     roll = lax.axis_index("roll")
     mach = lax.axis_index("mach")
     cross = lax.axis_index("cross")
@@ -190,9 +190,15 @@
     total = recv_b[0]
     for p in range(1, group_b):
         total = total + recv_b[p]
-    total_s[...] = total * scale
-    for r in range(rank):
-        mode_ref[r : r + 1, :] = total_s[r // per_row : r // per_row + 1, (r % per_row) * span : (r % per_row + 1) * span]
+    mode_ref[...] = total * scale
+
+
+def finish_kernel(rf_ref, total_ref, rf_out, mode_out):
+    rf_out[...] = rf_ref[...]
+    span = mode_out.shape[1]
+    per_row = 128 // span
+    for r in range(mode_out.shape[0]):
+        mode_out[r : r + 1, :] = total_ref[r // per_row : r // per_row + 1, (r % per_row) * span : (r % per_row + 1) * span]
 
 
 def local(density, roll_start, mach_factor, cross_factor):
@@ -209,7 +215,7 @@
         functools.partial(fused_kernel, n_roll, n_cross, scale, n_chunks),
         out_shape=(
             jax.ShapeDtypeStruct(roll_start.shape, jnp.float32),
-            jax.ShapeDtypeStruct((rank, span), jnp.float32),
+            jax.ShapeDtypeStruct((rank * span // 128, 128), jnp.float32),
         ),
         in_specs=[pl.BlockSpec(memory_space=pl.ANY)] + [pl.BlockSpec(memory_space=VMEM)] * 3,
         out_specs=[pl.BlockSpec(memory_space=VMEM)] * 2,
@@ -234,11 +240,18 @@
             VMEM((n_roll * n_cross, rank * span // 128, 128), jnp.float32),
             pltpu.SemaphoreType.DMA((n_roll * n_cross,)),
             pltpu.SemaphoreType.DMA((n_roll * n_cross,)),
-            VMEM((rank * span // 128, 128), jnp.float32),
         ],
         compiler_params=pltpu.CompilerParams(collective_id=0, has_side_effects=True),
     )(density, cross_factor, mach_factor, roll_start)
-    return (roll_factor, mode_two)
+    return pl.pallas_call(
+        finish_kernel,
+        out_shape=(
+            jax.ShapeDtypeStruct(roll_start.shape, jnp.float32),
+            jax.ShapeDtypeStruct((rank, span), jnp.float32),
+        ),
+        in_specs=[pl.BlockSpec(memory_space=VMEM)] * 2,
+        out_specs=[pl.BlockSpec(memory_space=VMEM)] * 2,
+    )(roll_factor, mode_two)
 
 
 def solution(mesh):

time: 32.6 us -> 31.1 us (0.954)
  local copies, waits for them, and re-layouts: 2.65 us -> 0 us
  Pallas kernels: 28.9 us -> 30.2 us
    unnamed x2 -> x0, local copies, waits for them, and re-layouts: 2.65 us -> none
    pallas_call x0 -> x1, Pallas kernels: none -> 1.41 us  [local(): pl.pallas_call(finish_kernel, out_shape=(jax.ShapeDtypeStruct(roll_start....]
where the time goes in v9:
time: 31.1 us; the launch traced here: 30.8 us
  Pallas kernels  30.2 us (97%)
  between operations  0.64 us (2%)
    pallas_call x1, Pallas kernels, local(): pl.pallas_call(functools.partial(fused_kernel, n_roll, n_cross, scale, n_...  28.8 us
    pallas_call x1, Pallas kernels, local(): pl.pallas_call(finish_kernel, out_shape=(jax.ShapeDtypeStruct(roll_start....  1.41 us

profile of v9, /device:TPU:1, one launch (start us, length us, event | category | flops | bytes accessed | tf_op | source)
XLA Modules:
  0.0 30.8 jit_solution(16017242137594689240)
XLA Ops:
  0.6 28.8 %shard_map.59 = (f32[32,32]{1,0:T(8,128)}, f32[16,128]{1,0:T(8,128)}) custom-call(bf16[32,256,512]{2,1,0:T(8,128)(2,1)} %dens_hbm.1, bf16[32,512]{1,0:T(8,128)(2,1)} %cross_ref.1, bf16[32,256]{1,0:T(8,128)(2,1)} %mach_ref.1, f32[32,32]{1,0:T(8,128)} %start_ref.1), custom_call_target="tpu_custom_call" | custom-call | tf_op jit(solution)/shard_map/pallas_call | solution.py:214
  29.4 1.4 %shard_map.60 = (f32[32,32]{1,0:T(8,128)}, f32[32,64]{1,0:T(8,128)}) custom-call(f32[32,32]{1,0:T(8,128)} %get-tuple-element.4.rf_ref, f32[16,128]{1,0:T(8,128)} %get-tuple-element.5.total_ref), custom_call_target="tpu_custom_call" | custom-call | tf_op jit(solution)/shard_map/pallas_call | solution.py:246

commit v10 on v9

--- a/solution.py
+++ b/solution.py
@@ -54,12 +54,14 @@
             pl.semaphore_signal(barrier, inc=1, device_id=peer_b(p), device_id_type=MESH)
         return carry
 
-    lax.fori_loop(0, n_mach, greet_m, 0)
+    for p in range(n_mach):
+        greet_m(p, 0)
     for p in range(n_cross):
         @pl.when(p != cross)
         def _():
             pl.semaphore_signal(barrier, inc=1, device_id=peer_c(p), device_id_type=MESH)
-    lax.fori_loop(0, group_b, greet_b, 0)
+    for p in range(group_b):
+        greet_b(p, 0)
 
     nt = (((1,), (1,)), ((), ()))
     cross_f = cross_ref[...]
@@ -127,9 +129,11 @@
                 device_id=peer_m(p), device_id_type=MESH).wait()
         return carry
 
-    lax.fori_loop(0, n_mach, send_loop_2, 0)
+    for p in range(n_mach):
+        send_loop_2(p, 0)
     recv_2[mach] = pay_2[...]
-    lax.fori_loop(0, n_mach, wait_loop_2, 0)
+    for p in range(n_mach):
+        wait_loop_2(p, 0)
     gm = recv_2[0, 0:8, :]
     terms = recv_2[0, 8:16, :]
     for p in range(1, n_mach):
@@ -154,16 +158,19 @@
         mixed = mixed + gram[:, r : r + 1] * (updated - current)
 
     factor = rf_ref[...]
+    bins_here_k = term_s.shape[0] * 128
     term = part_ref[0] * factor[:, 0:1]
     for i in range(1, part_ref.shape[0]):
         term = term + part_ref[i] * factor[:, i : i + 1]
-    term_s[...] = term
-    span = term_s.shape[1] // n_cross
+    for t in range(term_s.shape[0]):
+        term_s[t] = term[:, t * 128 : (t + 1) * 128]
+    span = bins_here_k // n_cross
     per_row = 128 // span
     for c in range(n_cross):
-        for r in range(rank):
-            pieces[c, r // per_row : r // per_row + 1, (r % per_row) * span : (r % per_row + 1) * span] = (
-                term_s[r : r + 1, c * span : (c + 1) * span])
+        lo = (c * span) % 128
+        for h in range(per_row):
+            rows = term_s[(c * span) // 128, pl.ds(h, rank // per_row, stride=per_row), :]
+            pieces[c, :, h * span : (h + 1) * span] = rows[:, lo : lo + span]
 
     def send_loop_b(p, carry):
         @pl.when(p != me_b)
@@ -183,9 +190,11 @@
             ).wait()
         return carry
 
-    lax.fori_loop(0, group_b, send_loop_b, 0)
+    for p in range(group_b):
+        send_loop_b(p, 0)
     recv_b[me_b] = pieces[cross]
-    lax.fori_loop(0, group_b, wait_loop_b, 0)
+    for p in range(group_b):
+        wait_loop_b(p, 0)
 
     total = recv_b[0]
     for p in range(1, group_b):
@@ -235,7 +244,7 @@
             VMEM((rank, rank), jnp.float32),
             VMEM((rank, rank), jnp.float32),
             VMEM((rank, rank), jnp.float32),
-            VMEM((rank, bins_here), jnp.float32),
+            VMEM((bins_here // 128, rank, 128), jnp.float32),
             VMEM((n_cross, rank * span // 128, 128), jnp.float32),
             VMEM((n_roll * n_cross, rank * span // 128, 128), jnp.float32),
             pltpu.SemaphoreType.DMA((n_roll * n_cross,)),

time: 31.1 us -> 31 us (level)
  no operation moved by 1% of the time
where the time goes in v10:
time: 31 us; the launch traced here: 30.7 us
  Pallas kernels  30 us (97%)
  between operations  0.64 us (2%)
    pallas_call x1, Pallas kernels, local(): pl.pallas_call(functools.partial(fused_kernel, n_roll, n_cross, scale, n_...  28.6 us
    pallas_call x1, Pallas kernels, local(): pl.pallas_call(finish_kernel, out_shape=(jax.ShapeDtypeStruct(roll_start....  1.41 us

profile of v10, /device:TPU:1, one launch (start us, length us, event | category | flops | bytes accessed | tf_op | source)
XLA Modules:
  0.0 30.7 jit_solution(15277980941025559562)
XLA Ops:
  0.6 28.6 %shard_map.59 = (f32[32,32]{1,0:T(8,128)}, f32[16,128]{1,0:T(8,128)}) custom-call(bf16[32,256,512]{2,1,0:T(8,128)(2,1)} %dens_hbm.1, bf16[32,512]{1,0:T(8,128)(2,1)} %cross_ref.1, bf16[32,256]{1,0:T(8,128)(2,1)} %mach_ref.1, f32[32,32]{1,0:T(8,128)} %start_ref.1), custom_call_target="tpu_custom_call" | custom-call | tf_op jit(solution)/shard_map/pallas_call | solution.py:223
  29.3 1.4 %shard_map.60 = (f32[32,32]{1,0:T(8,128)}, f32[32,64]{1,0:T(8,128)}) custom-call(f32[32,32]{1,0:T(8,128)} %get-tuple-element.4.rf_ref, f32[16,128]{1,0:T(8,128)} %get-tuple-element.5.total_ref), custom_call_target="tpu_custom_call" | custom-call | tf_op jit(solution)/shard_map/pallas_call | solution.py:255

commit v11 on v10

--- a/solution.py
+++ b/solution.py
@@ -9,6 +9,10 @@
 
 MESH = pl.DeviceIdType.MESH
 VMEM = pltpu.VMEM
+
+
+def far_first(n):
+    return sorted(range(1, n), key=lambda d: -min(d, n - d))
 
 
 def fused_kernel(n_roll, n_cross, scale, n_chunks, dens_hbm, cross_ref, mach_ref, start_ref, rf_ref, mode_ref,
@@ -95,10 +99,8 @@
             src_ref=pay_ref.at[pl.ds(8, 16)], dst_ref=recv_1.at[p], send_sem=send_1.at[p],
             recv_sem=got_1.at[p], device_id=peer_c(p), device_id_type=MESH)
 
-    for p in range(n_cross):
-        @pl.when(p != cross)
-        def _():
-            stage_1(p).start()
+    for dc in far_first(n_cross):
+        stage_1((cross + dc) % n_cross).start()
     recv_1[cross] = pay_ref[8:24, :]
     for p in range(n_cross):
         @pl.when(p != cross)
@@ -113,14 +115,6 @@
     pay_2[0:8, :] = pay_ref[0:8, :]
     pay_2[8:16, :] = terms
 
-    def send_loop_2(p, carry):
-        @pl.when(p != mach)
-        def _():
-            pltpu.make_async_remote_copy(
-                src_ref=pay_2, dst_ref=recv_2.at[mach], send_sem=send_2.at[p], recv_sem=got_2.at[mach],
-                device_id=peer_m(p), device_id_type=MESH).start()
-        return carry
-
     def wait_loop_2(p, carry):
         @pl.when(p != mach)
         def _():
@@ -129,8 +123,15 @@
                 device_id=peer_m(p), device_id_type=MESH).wait()
         return carry
 
-    for p in range(n_mach):
-        send_loop_2(p, 0)
+    n_x = 4 if n_mach % 4 == 0 else n_mach
+    n_y = n_mach // n_x
+    offsets = [(dy, dx) for dy in range(n_y) for dx in range(n_x) if (dy, dx) != (0, 0)]
+    offsets.sort(key=lambda o: -(min(o[0], n_y - o[0]) + min(o[1], n_x - o[1])))
+    for dy, dx in offsets:
+        p = ((mach // n_x + dy) % n_y) * n_x + (mach % n_x + dx) % n_x
+        pltpu.make_async_remote_copy(
+            src_ref=pay_2, dst_ref=recv_2.at[mach], send_sem=send_2.at[p], recv_sem=got_2.at[mach],
+            device_id=peer_m(p), device_id_type=MESH).start()
     recv_2[mach] = pay_2[...]
     for p in range(n_mach):
         wait_loop_2(p, 0)
@@ -151,9 +152,10 @@
     mixed = gram[:, 0:1] * rows[0:1, :]
     for s_ in range(1, rank):
         mixed = mixed + gram[:, s_ : s_ + 1] * rows[s_ : s_ + 1, :]
+    inverse = 1.0 / gram
     for r in range(rank):
         current = rows[r : r + 1, :]
-        updated = jnp.maximum(current + (target[r : r + 1, :] - mixed[r : r + 1, :]) / gram[r : r + 1, r : r + 1], 0.0)
+        updated = jnp.maximum(current + (target[r : r + 1, :] - mixed[r : r + 1, :]) * inverse[r : r + 1, r : r + 1], 0.0)
         rf_ref[r : r + 1, :] = updated
         mixed = mixed + gram[:, r : r + 1] * (updated - current)
 
@@ -172,15 +174,6 @@
             rows = term_s[(c * span) // 128, pl.ds(h, rank // per_row, stride=per_row), :]
             pieces[c, :, h * span : (h + 1) * span] = rows[:, lo : lo + span]
 
-    def send_loop_b(p, carry):
-        @pl.when(p != me_b)
-        def _():
-            pltpu.make_async_remote_copy(
-                src_ref=pieces.at[p % n_cross], dst_ref=recv_b.at[me_b],
-                send_sem=send_b.at[p], recv_sem=got_b.at[me_b], device_id=peer_b(p), device_id_type=MESH,
-            ).start()
-        return carry
-
     def wait_loop_b(p, carry):
         @pl.when(p != me_b)
         def _():
@@ -190,8 +183,15 @@
             ).wait()
         return carry
 
-    for p in range(group_b):
-        send_loop_b(p, 0)
+    for dc in [d for d in far_first(n_cross)] + [0]:
+        for da in range(n_roll):
+            if (da, dc) == (0, 0):
+                continue
+            p = ((roll + da) % n_roll) * n_cross + (cross + dc) % n_cross
+            pltpu.make_async_remote_copy(
+                src_ref=pieces.at[(cross + dc) % n_cross], dst_ref=recv_b.at[me_b],
+                send_sem=send_b.at[p], recv_sem=got_b.at[me_b], device_id=peer_b(p), device_id_type=MESH,
+            ).start()
     recv_b[me_b] = pieces[cross]
     for p in range(group_b):
         wait_loop_b(p, 0)

time: 31 us -> 31.8 us (1.026)
  Pallas kernels: 30 us -> 30.8 us
    pallas_call x1, Pallas kernels: 28.6 us -> 29.4 us  [local(): pl.pallas_call(functools.partial(fused_kernel, n_roll, n_cross, scale, n_...]
where the time goes in v11:
time: 31.8 us; the launch traced here: 31.4 us
  Pallas kernels  30.8 us (97%)
  between operations  0.64 us (2%)
    pallas_call x1, Pallas kernels, local(): pl.pallas_call(functools.partial(fused_kernel, n_roll, n_cross, scale, n_...  29.4 us
    pallas_call x1, Pallas kernels, local(): pl.pallas_call(finish_kernel, out_shape=(jax.ShapeDtypeStruct(roll_start....  1.41 us

profile of v11, /device:TPU:1, one launch (start us, length us, event | category | flops | bytes accessed | tf_op | source)
XLA Modules:
  0.0 31.4 jit_solution(9511828009875990654)
XLA Ops:
  0.6 29.4 %shard_map.59 = (f32[32,32]{1,0:T(8,128)}, f32[16,128]{1,0:T(8,128)}) custom-call(bf16[32,256,512]{2,1,0:T(8,128)(2,1)} %dens_hbm.1, bf16[32,512]{1,0:T(8,128)(2,1)} %cross_ref.1, bf16[32,256]{1,0:T(8,128)(2,1)} %mach_ref.1, f32[32,32]{1,0:T(8,128)} %start_ref.1), custom_call_target="tpu_custom_call" | custom-call | tf_op jit(solution)/shard_map/pallas_call | solution.py:223
  30.0 1.4 %shard_map.60 = (f32[32,32]{1,0:T(8,128)}, f32[32,64]{1,0:T(8,128)}) custom-call(f32[32,32]{1,0:T(8,128)} %get-tuple-element.4.rf_ref, f32[16,128]{1,0:T(8,128)} %get-tuple-element.5.total_ref), custom_call_target="tpu_custom_call" | custom-call | tf_op jit(solution)/shard_map/pallas_call | solution.py:255

commit v12 on v10

--- a/solution.py
+++ b/solution.py
@@ -151,9 +151,10 @@
     mixed = gram[:, 0:1] * rows[0:1, :]
     for s_ in range(1, rank):
         mixed = mixed + gram[:, s_ : s_ + 1] * rows[s_ : s_ + 1, :]
+    inverse = 1.0 / gram
     for r in range(rank):
         current = rows[r : r + 1, :]
-        updated = jnp.maximum(current + (target[r : r + 1, :] - mixed[r : r + 1, :]) / gram[r : r + 1, r : r + 1], 0.0)
+        updated = jnp.maximum(current + (target[r : r + 1, :] - mixed[r : r + 1, :]) * inverse[r : r + 1, r : r + 1], 0.0)
         rf_ref[r : r + 1, :] = updated
         mixed = mixed + gram[:, r : r + 1] * (updated - current)
 

time: 31 us -> 31 us (level)
  no operation moved by 1% of the time
where the time goes in v12:
time: 31 us; the launch traced here: 30.7 us
  Pallas kernels  30.1 us (97%)
  between operations  0.64 us (2%)
    pallas_call x1, Pallas kernels, local(): pl.pallas_call(functools.partial(fused_kernel, n_roll, n_cross, scale, n_...  28.7 us
    pallas_call x1, Pallas kernels, local(): pl.pallas_call(finish_kernel, out_shape=(jax.ShapeDtypeStruct(roll_start....  1.41 us

profile of v12, /device:TPU:1, one launch (start us, length us, event | category | flops | bytes accessed | tf_op | source)
XLA Modules:
  0.0 30.7 jit_solution(11947467332732884172)
XLA Ops:
  0.6 28.7 %shard_map.59 = (f32[32,32]{1,0:T(8,128)}, f32[16,128]{1,0:T(8,128)}) custom-call(bf16[32,256,512]{2,1,0:T(8,128)(2,1)} %dens_hbm.1, bf16[32,512]{1,0:T(8,128)(2,1)} %cross_ref.1, bf16[32,256]{1,0:T(8,128)(2,1)} %mach_ref.1, f32[32,32]{1,0:T(8,128)} %start_ref.1), custom_call_target="tpu_custom_call" | custom-call | tf_op jit(solution)/shard_map/pallas_call | solution.py:224
  29.3 1.4 %shard_map.60 = (f32[32,32]{1,0:T(8,128)}, f32[32,64]{1,0:T(8,128)}) custom-call(f32[32,32]{1,0:T(8,128)} %get-tuple-element.4.rf_ref, f32[16,128]{1,0:T(8,128)} %get-tuple-element.5.total_ref), custom_call_target="tpu_custom_call" | custom-call | tf_op jit(solution)/shard_map/pallas_call | solution.py:256

commit v13 on v10

--- a/solution.py
+++ b/solution.py
@@ -11,8 +11,8 @@
 VMEM = pltpu.VMEM
 
 
-def fused_kernel(n_roll, n_cross, scale, n_chunks, dens_hbm, cross_ref, mach_ref, start_ref, rf_ref, mode_ref,
-                 dens_v, dens_sem, part_ref, local_s, pay_ref,
+def fused_kernel(n_roll, n_cross, scale, n_chunks, dens_hbm, cross_hbm, mach_hbm, start_hbm, rf_ref, mode_ref,
+                 cross_ref, mach_ref, start_ref, small_sem, dens_v, dens_sem, part_ref, local_s, pay_ref,
                  recv_1, send_1, got_1, pay_2, recv_2, send_2, got_2, gm_s, mt_s, gc_s, term_s, pieces, recv_b, send_b, got_b):
     roll = lax.axis_index("roll")
     mach = lax.axis_index("mach")
@@ -37,8 +37,15 @@
         pltpu.make_async_copy(dens_hbm.at[pl.ds(k * chunk, chunk)], dens_v.at[pl.ds(k * chunk, chunk)], dens_sem.at[k])
         for k in range(n_chunks)
     ]
+    small = [
+        pltpu.make_async_copy(src, dst, small_sem.at[k])
+        for k, (src, dst) in enumerate(((cross_hbm, cross_ref), (mach_hbm, mach_ref), (start_hbm, start_ref)))
+    ]
+    small[0].start()
     for load in loads:
         load.start()
+    small[1].start()
+    small[2].start()
 
     barrier = pltpu.get_barrier_semaphore()
 
@@ -64,6 +71,8 @@
         greet_b(p, 0)
 
     nt = (((1,), (1,)), ((), ()))
+    small[0].wait()
+    small[1].wait()
     cross_f = cross_ref[...]
     mach_f = mach_ref[...]
     mach_w = mach_f.astype(jnp.float32)
@@ -147,6 +156,7 @@
 
     gram = gm_s[...] * gc_s[...]
     target = mt_s[...]
+    small[2].wait()
     rows = start_ref[...]
     mixed = gram[:, 0:1] * rows[0:1, :]
     for s_ in range(1, rank):
@@ -226,9 +236,13 @@
             jax.ShapeDtypeStruct(roll_start.shape, jnp.float32),
             jax.ShapeDtypeStruct((rank * span // 128, 128), jnp.float32),
         ),
-        in_specs=[pl.BlockSpec(memory_space=pl.ANY)] + [pl.BlockSpec(memory_space=VMEM)] * 3,
+        in_specs=[pl.BlockSpec(memory_space=pl.ANY)] * 4,
         out_specs=[pl.BlockSpec(memory_space=VMEM)] * 2,
         scratch_shapes=[
+            VMEM(cross_factor.shape, cross_factor.dtype),
+            VMEM(mach_factor.shape, mach_factor.dtype),
+            VMEM(roll_start.shape, roll_start.dtype),
+            pltpu.SemaphoreType.DMA((3,)),
             VMEM(density.shape, density.dtype),
             pltpu.SemaphoreType.DMA((n_chunks,)),
             VMEM((rolls_here, rank, bins_here), jnp.float32),

time: 31 us -> 31.5 us (1.016)
  Pallas kernels: 30 us -> 30.7 us
    pallas_call x1, Pallas kernels: 28.6 us -> 29.3 us  [local(): pl.pallas_call(functools.partial(fused_kernel, n_roll, n_cross, scale, n_...]
where the time goes in v13:
time: 31.5 us; the launch traced here: 31.3 us
  Pallas kernels  30.7 us (97%)
  between operations  0.64 us (2%)
    pallas_call x1, Pallas kernels, local(): pl.pallas_call(functools.partial(fused_kernel, n_roll, n_cross, scale, n_...  29.3 us
    pallas_call x1, Pallas kernels, local(): pl.pallas_call(finish_kernel, out_shape=(jax.ShapeDtypeStruct(roll_start....  1.41 us

profile of v13, /device:TPU:1, one launch (start us, length us, event | category | flops | bytes accessed | tf_op | source)
XLA Modules:
  0.0 31.3 jit_solution(9809427531835222089)
XLA Ops:
  0.6 29.3 %shard_map.59 = (f32[32,32]{1,0:T(8,128)}, f32[16,128]{1,0:T(8,128)}) custom-call(bf16[32,256,512]{2,1,0:T(8,128)(2,1)} %dens_hbm.1, bf16[32,512]{1,0:T(8,128)(2,1)} %cross_hbm.1, bf16[32,256]{1,0:T(8,128)(2,1)} %mach_hbm.1, f32[32,32]{1,0:T(8,128)} %start_hbm.1), custom_call_target="tpu_custom_call" | custom-call | tf_op jit(solution)/shard_map/pallas_call | solution.py:233
  29.9 1.4 %shard_map.60 = (f32[32,32]{1,0:T(8,128)}, f32[32,64]{1,0:T(8,128)}) custom-call(f32[32,32]{1,0:T(8,128)} %get-tuple-element.4.rf_ref, f32[16,128]{1,0:T(8,128)} %get-tuple-element.5.total_ref), custom_call_target="tpu_custom_call" | custom-call | tf_op jit(solution)/shard_map/pallas_call | solution.py:269

commit v14 on v10

--- a/solution.py
+++ b/solution.py
@@ -13,13 +13,17 @@
 
 def fused_kernel(n_roll, n_cross, scale, n_chunks, dens_hbm, cross_ref, mach_ref, start_ref, rf_ref, mode_ref,
                  dens_v, dens_sem, part_ref, local_s, pay_ref,
-                 recv_1, send_1, got_1, pay_2, recv_2, send_2, got_2, gm_s, mt_s, gc_s, term_s, pieces, recv_b, send_b, got_b):
+                 recv_1, send_1, got_1, pay_2, recv_2, send_2, got_2, gm_s, mt_s, gc_s, term_s, pieces,
+                 recv_b1, send_b1, got_b1, core_sum, recv_b2, send_b2, got_b2):
     roll = lax.axis_index("roll")
     mach = lax.axis_index("mach")
     cross = lax.axis_index("cross")
     n_mach = recv_2.shape[0]
-    group_b = recv_b.shape[0]
-    me_b = roll * n_cross + cross
+    n_core = recv_b1.shape[0]
+    n_zl = recv_b2.shape[0] // n_cross
+    zl = roll // n_core
+    core = roll % n_core
+    me_z = zl * n_cross + cross
     rank = rf_ref.shape[0]
 
     def peer_c(p):
@@ -28,8 +32,11 @@
     def peer_m(p):
         return (roll, p, cross)
 
-    def peer_b(p):
-        return (p // n_cross, mach, p % n_cross)
+    def peer_core(q):
+        return (zl * n_core + q, mach, cross)
+
+    def peer_z(p):
+        return ((p // n_cross) * n_core + core, mach, p % n_cross)
 
     rolls_here = dens_v.shape[0]
     chunk = rolls_here // n_chunks
@@ -49,9 +56,9 @@
         return carry
 
     def greet_b(p, carry):
-        @pl.when(p // n_cross != roll)
-        def _():
-            pl.semaphore_signal(barrier, inc=1, device_id=peer_b(p), device_id_type=MESH)
+        @pl.when(p // n_cross != zl)
+        def _():
+            pl.semaphore_signal(barrier, inc=1, device_id=peer_z(p), device_id_type=MESH)
         return carry
 
     for p in range(n_mach):
@@ -60,8 +67,12 @@
         @pl.when(p != cross)
         def _():
             pl.semaphore_signal(barrier, inc=1, device_id=peer_c(p), device_id_type=MESH)
-    for p in range(group_b):
+    for p in range(n_zl * n_cross):
         greet_b(p, 0)
+    for q in range(n_core):
+        @pl.when(q != core)
+        def _():
+            pl.semaphore_signal(barrier, inc=1, device_id=peer_core(q), device_id_type=MESH)
 
     nt = (((1,), (1,)), ((), ()))
     cross_f = cross_ref[...]
@@ -83,7 +94,7 @@
         for g in range(4):
             pay_ref[8 * k : 8 * k + 8, g * 32 : (g + 1) * 32] = local_s[k, pl.ds(g, 8, stride=4), :]
 
-    pl.semaphore_wait(barrier, n_mach - 1 + group_b - 1)
+    pl.semaphore_wait(barrier, n_mach - 1 + n_cross - 1 + n_core - 1 + (n_zl - 1) * n_cross)
 
     def stage_1(p):
         return pltpu.make_async_remote_copy(
@@ -172,33 +183,41 @@
             rows = term_s[(c * span) // 128, pl.ds(h, rank // per_row, stride=per_row), :]
             pieces[c, :, h * span : (h + 1) * span] = rows[:, lo : lo + span]
 
-    def send_loop_b(p, carry):
-        @pl.when(p != me_b)
-        def _():
-            pltpu.make_async_remote_copy(
-                src_ref=pieces.at[p % n_cross], dst_ref=recv_b.at[me_b],
-                send_sem=send_b.at[p], recv_sem=got_b.at[me_b], device_id=peer_b(p), device_id_type=MESH,
-            ).start()
-        return carry
-
-    def wait_loop_b(p, carry):
-        @pl.when(p != me_b)
-        def _():
-            pltpu.make_async_remote_copy(
-                src_ref=pieces.at[p % n_cross], dst_ref=recv_b.at[p],
-                send_sem=send_b.at[p], recv_sem=got_b.at[p], device_id=peer_b(p), device_id_type=MESH,
-            ).wait()
-        return carry
-
-    for p in range(group_b):
-        send_loop_b(p, 0)
-    recv_b[me_b] = pieces[cross]
-    for p in range(group_b):
-        wait_loop_b(p, 0)
-
-    total = recv_b[0]
-    for p in range(1, group_b):
-        total = total + recv_b[p]
+    for q in range(n_core):
+        @pl.when(q != core)
+        def _():
+            pltpu.make_async_remote_copy(
+                src_ref=pieces, dst_ref=recv_b1.at[core], send_sem=send_b1.at[q], recv_sem=got_b1.at[core],
+                device_id=peer_core(q), device_id_type=MESH).start()
+    recv_b1[core] = pieces[...]
+    for q in range(n_core):
+        @pl.when(q != core)
+        def _():
+            pltpu.make_async_remote_copy(
+                src_ref=pieces, dst_ref=recv_b1.at[q], send_sem=send_b1.at[q], recv_sem=got_b1.at[q],
+                device_id=peer_core(q), device_id_type=MESH).wait()
+    summed = recv_b1[0]
+    for q in range(1, n_core):
+        summed = summed + recv_b1[q]
+    core_sum[...] = summed
+
+    for p in range(n_zl * n_cross):
+        @pl.when(p != me_z)
+        def _():
+            pltpu.make_async_remote_copy(
+                src_ref=core_sum.at[p % n_cross], dst_ref=recv_b2.at[me_z], send_sem=send_b2.at[p],
+                recv_sem=got_b2.at[me_z], device_id=peer_z(p), device_id_type=MESH).start()
+    recv_b2[me_z] = core_sum[cross]
+    for p in range(n_zl * n_cross):
+        @pl.when(p != me_z)
+        def _():
+            pltpu.make_async_remote_copy(
+                src_ref=core_sum.at[p % n_cross], dst_ref=recv_b2.at[p], send_sem=send_b2.at[p],
+                recv_sem=got_b2.at[p], device_id=peer_z(p), device_id_type=MESH).wait()
+
+    total = recv_b2[0]
+    for p in range(1, n_zl * n_cross):
+        total = total + recv_b2[p]
     mode_ref[...] = total * scale
 
 
@@ -217,6 +236,7 @@
     n_mach = lax.axis_size("mach")
     n_cross = lax.axis_size("cross")
     n_chunks = 4
+    n_core = 2 if n_roll % 2 == 0 else 1
     pay_rows = 3 * rank * rank // 128
     span = bins_here // n_cross
     scale = rank / (rolls_here * n_roll * cross_here * n_cross)
@@ -246,9 +266,13 @@
             VMEM((rank, rank), jnp.float32),
             VMEM((bins_here // 128, rank, 128), jnp.float32),
             VMEM((n_cross, rank * span // 128, 128), jnp.float32),
-            VMEM((n_roll * n_cross, rank * span // 128, 128), jnp.float32),
-            pltpu.SemaphoreType.DMA((n_roll * n_cross,)),
-            pltpu.SemaphoreType.DMA((n_roll * n_cross,)),
+            VMEM((n_core, n_cross, rank * span // 128, 128), jnp.float32),
+            pltpu.SemaphoreType.DMA((n_core,)),
+            pltpu.SemaphoreType.DMA((n_core,)),
+            VMEM((n_cross, rank * span // 128, 128), jnp.float32),
+            VMEM((n_roll // n_core * n_cross, rank * span // 128, 128), jnp.float32),
+            pltpu.SemaphoreType.DMA((n_roll // n_core * n_cross,)),
+            pltpu.SemaphoreType.DMA((n_roll // n_core * n_cross,)),
         ],
         compiler_params=pltpu.CompilerParams(collective_id=0, has_side_effects=True),
     )(density, cross_factor, mach_factor, roll_start)

time: 31 us -> 31.3 us (level)
  no operation moved by 1% of the time
where the time goes in v14:
time: 31.3 us; the launch traced here: 31 us
  Pallas kernels  30.3 us (97%)
  between operations  0.64 us (2%)
    pallas_call x1, Pallas kernels, local(): pl.pallas_call(functools.partial(fused_kernel, n_roll, n_cross, scale, n_...  28.9 us
    pallas_call x1, Pallas kernels, local(): pl.pallas_call(finish_kernel, out_shape=(jax.ShapeDtypeStruct(roll_start....  1.41 us

profile of v14, /device:TPU:1, one launch (start us, length us, event | category | flops | bytes accessed | tf_op | source)
XLA Modules:
  0.0 31.0 jit_solution(5605632354180188199)
XLA Ops:
  0.6 28.9 %shard_map.59 = (f32[32,32]{1,0:T(8,128)}, f32[16,128]{1,0:T(8,128)}) custom-call(bf16[32,256,512]{2,1,0:T(8,128)(2,1)} %dens_hbm.1, bf16[32,512]{1,0:T(8,128)(2,1)} %cross_ref.1, bf16[32,256]{1,0:T(8,128)(2,1)} %mach_ref.1, f32[32,32]{1,0:T(8,128)} %start_ref.1), custom_call_target="tpu_custom_call" | custom-call | tf_op jit(solution)/shard_map/pallas_call | solution.py:243
  29.6 1.4 %shard_map.60 = (f32[32,32]{1,0:T(8,128)}, f32[32,64]{1,0:T(8,128)}) custom-call(f32[32,32]{1,0:T(8,128)} %get-tuple-element.4.rf_ref, f32[16,128]{1,0:T(8,128)} %get-tuple-element.5.total_ref), custom_call_target="tpu_custom_call" | custom-call | tf_op jit(solution)/shard_map/pallas_call | solution.py:279

commit v15 on v10

--- a/solution.py
+++ b/solution.py
@@ -151,19 +151,24 @@
     mixed = gram[:, 0:1] * rows[0:1, :]
     for s_ in range(1, rank):
         mixed = mixed + gram[:, s_ : s_ + 1] * rows[s_ : s_ + 1, :]
+    bins_here_k = term_s.shape[0] * 128
+
+    def term_block(lo):
+        factor = rf_ref[lo : lo + 8, :]
+        term = part_ref[0, lo : lo + 8, :] * factor[:, 0:1]
+        for i in range(1, part_ref.shape[0]):
+            term = term + part_ref[i, lo : lo + 8, :] * factor[:, i : i + 1]
+        for t in range(term_s.shape[0]):
+            term_s[t, lo : lo + 8, :] = term[:, t * 128 : (t + 1) * 128]
+
     for r in range(rank):
         current = rows[r : r + 1, :]
         updated = jnp.maximum(current + (target[r : r + 1, :] - mixed[r : r + 1, :]) / gram[r : r + 1, r : r + 1], 0.0)
         rf_ref[r : r + 1, :] = updated
         mixed = mixed + gram[:, r : r + 1] * (updated - current)
-
-    factor = rf_ref[...]
-    bins_here_k = term_s.shape[0] * 128
-    term = part_ref[0] * factor[:, 0:1]
-    for i in range(1, part_ref.shape[0]):
-        term = term + part_ref[i] * factor[:, i : i + 1]
-    for t in range(term_s.shape[0]):
-        term_s[t] = term[:, t * 128 : (t + 1) * 128]
+        if r % 8 == 7:
+            term_block(r - 7)
+
     span = bins_here_k // n_cross
     per_row = 128 // span
     for c in range(n_cross):

time: 31 us -> 31 us (level)
  no operation moved by 1% of the time
where the time goes in v15:
time: 31 us; the launch traced here: 30.7 us
  Pallas kernels  30.1 us (97%)
  between operations  0.64 us (2%)
    pallas_call x1, Pallas kernels, local(): pl.pallas_call(functools.partial(fused_kernel, n_roll, n_cross, scale, n_...  28.6 us
    pallas_call x1, Pallas kernels, local(): pl.pallas_call(finish_kernel, out_shape=(jax.ShapeDtypeStruct(roll_start....  1.41 us

profile of v15, /device:TPU:1, one launch (start us, length us, event | category | flops | bytes accessed | tf_op | source)
XLA Modules:
  0.0 30.7 jit_solution(7527670998735443664)
XLA Ops:
  0.6 28.6 %shard_map.59 = (f32[32,32]{1,0:T(8,128)}, f32[16,128]{1,0:T(8,128)}) custom-call(bf16[32,256,512]{2,1,0:T(8,128)(2,1)} %dens_hbm.1, bf16[32,512]{1,0:T(8,128)(2,1)} %cross_ref.1, bf16[32,256]{1,0:T(8,128)(2,1)} %mach_ref.1, f32[32,32]{1,0:T(8,128)} %start_ref.1), custom_call_target="tpu_custom_call" | custom-call | tf_op jit(solution)/shard_map/pallas_call | solution.py:228
  29.3 1.4 %shard_map.60 = (f32[32,32]{1,0:T(8,128)}, f32[32,64]{1,0:T(8,128)}) custom-call(f32[32,32]{1,0:T(8,128)} %get-tuple-element.4.rf_ref, f32[16,128]{1,0:T(8,128)} %get-tuple-element.5.total_ref), custom_call_target="tpu_custom_call" | custom-call | tf_op jit(solution)/shard_map/pallas_call | solution.py:260

commit v16 on v10

--- a/solution.py
+++ b/solution.py
@@ -199,15 +199,22 @@
     total = recv_b[0]
     for p in range(1, group_b):
         total = total + recv_b[p]
-    mode_ref[...] = total * scale
-
-
-def finish_kernel(rf_ref, total_ref, rf_out, mode_out):
-    rf_out[...] = rf_ref[...]
-    span = mode_out.shape[1]
+    total = total * scale
+    span = mode_ref.shape[1]
     per_row = 128 // span
-    for r in range(mode_out.shape[0]):
-        mode_out[r : r + 1, :] = total_ref[r // per_row : r // per_row + 1, (r % per_row) * span : (r % per_row + 1) * span]
+    for h in range(per_row):
+        mode_ref[pl.ds(h, rank // per_row, stride=per_row), :] = total[:, h * span : (h + 1) * span]
+
+
+def finish_kernel(rf_ref, mode_ref, rf_out, mode_out, sems):
+    copies = [
+        pltpu.make_async_copy(rf_ref, rf_out, sems.at[0]),
+        pltpu.make_async_copy(mode_ref, mode_out, sems.at[1]),
+    ]
+    for copy in copies:
+        copy.start()
+    for copy in copies:
+        copy.wait()
 
 
 def local(density, roll_start, mach_factor, cross_factor):
@@ -224,7 +231,7 @@
         functools.partial(fused_kernel, n_roll, n_cross, scale, n_chunks),
         out_shape=(
             jax.ShapeDtypeStruct(roll_start.shape, jnp.float32),
-            jax.ShapeDtypeStruct((rank * span // 128, 128), jnp.float32),
+            jax.ShapeDtypeStruct((rank, span), jnp.float32),
         ),
         in_specs=[pl.BlockSpec(memory_space=pl.ANY)] + [pl.BlockSpec(memory_space=VMEM)] * 3,
         out_specs=[pl.BlockSpec(memory_space=VMEM)] * 2,
@@ -258,8 +265,9 @@
             jax.ShapeDtypeStruct(roll_start.shape, jnp.float32),
             jax.ShapeDtypeStruct((rank, span), jnp.float32),
         ),
-        in_specs=[pl.BlockSpec(memory_space=VMEM)] * 2,
-        out_specs=[pl.BlockSpec(memory_space=VMEM)] * 2,
+        in_specs=[pl.BlockSpec(memory_space=pl.ANY)] * 2,
+        out_specs=[pl.BlockSpec(memory_space=pl.ANY)] * 2,
+        scratch_shapes=[pltpu.SemaphoreType.DMA((2,))],
     )(roll_factor, mode_two)
 
 

time: 31 us -> 31.7 us (1.023)
  Pallas kernels: 30 us -> 30.8 us
    pallas_call x1, Pallas kernels: 1.41 us -> 2.11 us  [local(): pl.pallas_call(finish_kernel, out_shape=(jax.ShapeDtypeStruct(roll_start....]
where the time goes in v16:
time: 31.7 us; the launch traced here: 31.5 us
  Pallas kernels  30.8 us (97%)
  between operations  0.64 us (2%)
    pallas_call x1, Pallas kernels, local(): pl.pallas_call(functools.partial(fused_kernel, n_roll, n_cross, scale, n_...  28.7 us
    pallas_call x1, Pallas kernels, local(): pl.pallas_call(finish_kernel, out_shape=(jax.ShapeDtypeStruct(roll_start....  2.11 us

profile of v16, /device:TPU:1, one launch (start us, length us, event | category | flops | bytes accessed | tf_op | source)
XLA Modules:
  0.0 31.5 jit_solution(8446632899261492205)
XLA Ops:
  0.6 28.7 %shard_map.59 = (f32[32,32]{1,0:T(8,128)}, f32[32,64]{1,0:T(8,128)}) custom-call(bf16[32,256,512]{2,1,0:T(8,128)(2,1)} %dens_hbm.1, bf16[32,512]{1,0:T(8,128)(2,1)} %cross_ref.1, bf16[32,256]{1,0:T(8,128)(2,1)} %mach_ref.1, f32[32,32]{1,0:T(8,128)} %start_ref.1), custom_call_target="tpu_custom_call" | custom-call | tf_op jit(solution)/shard_map/pallas_call | solution.py:230
  29.3 2.1 %shard_map.60 = (f32[32,32]{1,0:T(8,128)}, f32[32,64]{1,0:T(8,128)}) custom-call(f32[32,32]{1,0:T(8,128)} %get-tuple-element.4.rf_ref, f32[32,64]{1,0:T(8,128)} %get-tuple-element.5.mode_ref), custom_call_target="tpu_custom_call" | custom-call | tf_op jit(solution)/shard_map/pallas_call | solution.py:262

commit v17 on v10

--- a/solution.py
+++ b/solution.py
@@ -99,6 +99,12 @@
         @pl.when(p != cross)
         def _():
             stage_1(p).start()
+    for p in range(n_mach):
+        @pl.when(p != mach)
+        def _():
+            pltpu.make_async_remote_copy(
+                src_ref=pay_ref.at[pl.ds(0, 8)], dst_ref=recv_2.at[mach, pl.ds(0, 8)], send_sem=send_2.at[p],
+                recv_sem=got_2.at[mach], device_id=peer_m(p), device_id_type=MESH).start()
     recv_1[cross] = pay_ref[8:24, :]
     for p in range(n_cross):
         @pl.when(p != cross)
@@ -110,15 +116,14 @@
         terms = terms + recv_1[p, 0:8, :]
         gc = gc + recv_1[p, 8:16, :]
 
-    pay_2[0:8, :] = pay_ref[0:8, :]
     pay_2[8:16, :] = terms
 
     def send_loop_2(p, carry):
         @pl.when(p != mach)
         def _():
             pltpu.make_async_remote_copy(
-                src_ref=pay_2, dst_ref=recv_2.at[mach], send_sem=send_2.at[p], recv_sem=got_2.at[mach],
-                device_id=peer_m(p), device_id_type=MESH).start()
+                src_ref=pay_2.at[pl.ds(8, 8)], dst_ref=recv_2.at[mach, pl.ds(8, 8)], send_sem=send_2.at[p],
+                recv_sem=got_2.at[mach], device_id=peer_m(p), device_id_type=MESH).start()
         return carry
 
     def wait_loop_2(p, carry):
@@ -131,7 +136,8 @@
 
     for p in range(n_mach):
         send_loop_2(p, 0)
-    recv_2[mach] = pay_2[...]
+    recv_2[mach, 0:8, :] = pay_ref[0:8, :]
+    recv_2[mach, 8:16, :] = terms
     for p in range(n_mach):
         wait_loop_2(p, 0)
     gm = recv_2[0, 0:8, :]

time: 31 us -> 31 us (level)
  no operation moved by 1% of the time
where the time goes in v17:
time: 31 us; the launch traced here: 30.6 us
  Pallas kernels  30 us (97%)
  between operations  0.64 us (2%)
    pallas_call x1, Pallas kernels, local(): pl.pallas_call(functools.partial(fused_kernel, n_roll, n_cross, scale, n_...  28.6 us
    pallas_call x1, Pallas kernels, local(): pl.pallas_call(finish_kernel, out_shape=(jax.ShapeDtypeStruct(roll_start....  1.41 us

profile of v17, /device:TPU:1, one launch (start us, length us, event | category | flops | bytes accessed | tf_op | source)
XLA Modules:
  0.0 30.6 jit_solution(17055595645952701461)
XLA Ops:
  0.6 28.6 %shard_map.59 = (f32[32,32]{1,0:T(8,128)}, f32[16,128]{1,0:T(8,128)}) custom-call(bf16[32,256,512]{2,1,0:T(8,128)(2,1)} %dens_hbm.1, bf16[32,512]{1,0:T(8,128)(2,1)} %cross_ref.1, bf16[32,256]{1,0:T(8,128)(2,1)} %mach_ref.1, f32[32,32]{1,0:T(8,128)} %start_ref.1), custom_call_target="tpu_custom_call" | custom-call | tf_op jit(solution)/shard_map/pallas_call | solution.py:229
  29.2 1.4 %shard_map.60 = (f32[32,32]{1,0:T(8,128)}, f32[32,64]{1,0:T(8,128)}) custom-call(f32[32,32]{1,0:T(8,128)} %get-tuple-element.4.rf_ref, f32[16,128]{1,0:T(8,128)} %get-tuple-element.5.total_ref), custom_call_target="tpu_custom_call" | custom-call | tf_op jit(solution)/shard_map/pallas_call | solution.py:261
